TPU v7x, 128 devices: a whole 4x4x4 slice. The times are simulated.
128 devices in a mesh: group: 32 (over x, z, y_hi), grid: 4 (over y_lo, core).
Axes of the slice: x: 4, y: 4 (y_hi: 2, y_lo: 2; y = y_hi * 2 + y_lo), z: 4, core: 2. Of those that a mesh axis runs over, the one named last changes fastest.
Arguments:
- stochastic: bfloat16 [1024, 32, 1024], P('group', 'grid'), may hold values from -6 to 6
- plane_map: int32 [32, 1024], P('group'), may hold values from 0 to 1023, each once within a row
- core_orbitals: bfloat16 [32, 512, 32, 1024], P('group', None, 'grid'), may hold values from -0.03125 to 0.03125
- potential: float32 [32, 32, 1024], P('group', 'grid'), may hold values from 0 to 0.4
Outputs:
- density: float32 [32, 32, 1024], P('group', 'grid')
- own_filtered: float32 [1024, 32, 1024], P('group', 'grid')
Inputs may be any that keep to these rules, and one draw needn't show every extreme that they name: `plane_map`: each row names every plane point once.
All inputs are finite; a program needn't handle non-finite values.
Results may differ from a plain program's by a relative error of at most 0.001.
Values may be sent and summed in bfloat16 or wider, within the bound.
No kernel may reach another device: no remote copies, remote signals or barrier semaphores. Data moves between devices by JAX's collectives and lax.ppermute only.
A program may use at most 128 MiB of HBM per device.

v0:
```python
from fractions import Fraction

import jax
import jax.numpy as jnp
from jax import lax
from jax.experimental import pallas as pl
from jax.experimental.pallas import tpu as pltpu
from jax.sharding import PartitionSpec as P

BZ = 32
KDEG = 6
BATCH = 32
NCORE = 512
SLAB = 8
PLANE = 1024
GRID = 4
HALO = KDEG
WIDE = SLAB + 2 * HALO
LANES = 128
TILES = PLANE // LANES
F32 = jnp.float32
BF16 = jnp.bfloat16


def horner_coefficients():
    cheb = [[Fraction(1)], [Fraction(0), Fraction(1)]]
    for _ in range(2, KDEG + 1):
        last, before = cheb[-1], cheb[-2]
        nxt = [Fraction(0)] + [2 * v for v in last]
        for i, v in enumerate(before):
            nxt[i] -= v
        cheb.append(nxt)
    mono = [Fraction(0)] * (KDEG + 1)
    for k, poly in enumerate(cheb):
        for i, v in enumerate(poly):
            mono[i] += v / (k + 1)
    scaled = [v / Fraction(-8) ** i for i, v in enumerate(mono)]
    top = scaled[KDEG]
    return [float(v / top) for v in scaled], float(top)


EK, TOP = horner_coefficients()

VMEM = pl.BlockSpec(memory_space=pltpu.VMEM)
MIB = 1 << 20
PIECE = 32
CHUNKS = NCORE // PIECE
NT = (((1,), (1,)), ((), ()))


def call(kernel, name, out_shape, in_specs, scratch=(), limit=8):
    return pl.pallas_call(
        kernel,
        in_specs=in_specs,
        out_specs=jax.tree.map(lambda _: VMEM, out_shape),
        out_shape=out_shape,
        scratch_shapes=list(scratch),
        compiler_params=pltpu.CompilerParams(vmem_limit_bytes=limit * MIB),
        name=name,
    )


def struct(shape, dtype):
    return jax.ShapeDtypeStruct(shape, dtype)


def one_hot(condition):
    return jnp.where(condition, 1.0, 0.0).astype(BF16)


def iota(shape, axis):
    return lax.broadcasted_iota(jnp.int32, shape, axis)


def dot(a, b):
    return jnp.dot(a, b, preferred_element_type=F32)


def dot_nt(a, b):
    return lax.dot_general(a, b, NT, preferred_element_type=F32)


def row_permutation(rows, inner):
    outer = rows // inner
    out, src = iota((rows, rows), 0), iota((rows, rows), 1)
    return one_hot(src == (out % outer) * inner + out // outer)


def natural_point(q):
    tile, lane = q // LANES, q % LANES
    return (4 * (lane // 16) + tile // 2) * BZ + 2 * (lane % 16) + tile % 2


def prepare_kernel(index_ref, local_ref, below_ref, above_ref, order_ref, index_out, weight_out):
    order = one_hot(iota((PLANE, PLANE), 1) == natural_point(iota((PLANE, PLANE), 0)))
    order_ref[...] = order
    index = index_ref[...]
    digits = jnp.concatenate([index // 32, index % 32] + [jnp.zeros((6, PLANE), jnp.int32)], axis=0)
    moved = dot_nt(digits.astype(F32).astype(BF16), order)
    index_out[...] = (moved[0:1] * 32.0 + moved[1:2]).astype(jnp.int32)
    for first, ref in ((0, below_ref), (HALO, local_ref), (HALO + SLAB, above_ref)):
        rest = ref[...]
        total = None
        for _ in range(3):
            part = rest.astype(BF16)
            rest = rest - part.astype(F32)
            moved = dot_nt(part, order)
            total = moved if total is None else total + moved
        weight_out[first : first + ref.shape[0]] = 8.0 * total - 2.0


def prepare(plane_map, local, below, above):
    return call(
        prepare_kernel,
        "prepare",
        (
            struct((PLANE, PLANE), BF16),
            struct((1, PLANE), jnp.int32),
            struct((WIDE, PLANE), F32),
        ),
        [VMEM] * 4,
    )(plane_map, local, below, above)


def relayout_kernel(core_ref, out_ref, mid):
    rows = row_permutation(256, SLAB)
    src, out = iota((256, 256), 0), iota((256, 256), 1)
    piece, low = out // PIECE, out % PIECE
    columns = one_hot(src == (4 * (low // 16) + piece // 2) * BZ + 2 * (low % 16) + piece % 2)
    lane = iota((PIECE, LANES), 1)
    half, quarter = lane < 64, lane % 64 < 32

    @pl.loop(0, CHUNKS)
    def _(i):
        block = pl.ds(pl.multiple_of(i * 256, 256), 256)
        for b in range(4):
            cols = pl.ds(b * 256, 256)
            ordered = dot(rows, core_ref[block, cols]).astype(BF16)
            mid[:, cols] = dot(ordered, columns).astype(BF16)
        at = pl.ds(pl.multiple_of(i * PIECE, PIECE), PIECE)
        for x in range(SLAB):
            for h in range(2):
                p = [
                    mid[pl.ds(x * PIECE, PIECE), pl.ds(b * 256 + h * LANES, LANES)].astype(F32)
                    for b in range(4)
                ]
                u = [jnp.where(half, p[k], pltpu.roll(p[k + 2], 64, 1)) for k in range(2)]
                v = [jnp.where(half, pltpu.roll(p[k], 64, 1), p[k + 2]) for k in range(2)]
                for k, (a, c) in enumerate((u, v)):
                    first = jnp.where(quarter, a, pltpu.roll(c, 32, 1))
                    second = jnp.where(quarter, pltpu.roll(a, LANES - 32, 1), c)
                    j = 4 * h + 2 * k
                    out_ref[x, at, pl.ds(j * LANES, LANES)] = first.astype(BF16)
                    out_ref[x, at, pl.ds((j + 1) * LANES, LANES)] = second.astype(BF16)


def relayout(core):
    return call(
        relayout_kernel,
        "relayout",
        struct((SLAB, NCORE, PLANE), BF16),
        [VMEM],
        [pltpu.VMEM((256, PLANE), BF16)],
    )(core.reshape(NCORE * SLAB, PLANE))


def sums(field_of, core_ref, full_ref, half_ref):
    for x in range(SLAB):
        part = dot_nt(field_of(x), core_ref[x])
        if x == 0:
            full_ref[...] = part
        else:
            full_ref[...] += part
    half_ref[...] = full_ref[...].astype(BF16)


def map_kernel(*refs):
    index_ref, core_ref, batches = refs[0], refs[1], refs[2:-4]
    out_ref, full_ref, half_ref, pick = refs[-4:]
    pick[...] = one_hot(iota((PLANE, PLANE), 0) == index_ref[...])
    perm = row_permutation(BATCH * SLAB, SLAB)
    for b, ref in enumerate(batches):
        rows = dot(perm, ref[...]).astype(BF16)
        got = dot(rows, pick[...]).astype(BF16)
        out_ref[:, b * BATCH : (b + 1) * BATCH, :] = got.reshape(SLAB, BATCH, PLANE)
    sums(lambda x: out_ref[x], core_ref, full_ref, half_ref)


def map_batches(index_row, core_x, batches):
    rows = BATCH * len(batches)
    return call(
        map_kernel,
        "map_batches",
        (struct((SLAB, rows, PLANE), BF16), struct((rows, NCORE), F32), struct((rows, NCORE), BF16)),
        [VMEM] * (2 + len(batches)),
        [pltpu.VMEM((PLANE, PLANE), BF16)],
        limit=12,
    )(index_row, core_x, *[b.reshape(BATCH * SLAB, PLANE) for b in batches])


def exchange(half):
    return [
        lax.ppermute(half, "grid", [(i, i ^ k) for i in range(GRID)]) for k in range(1, GRID)
    ]


def total_of(full_ref, a_ref, b_ref, c_ref):
    rest = a_ref[...].astype(F32) + b_ref[...].astype(F32) + c_ref[...].astype(F32)
    return (full_ref[...] + rest).astype(BF16)


def project_kernel(full_ref, a_ref, b_ref, c_ref, field_ref, core_ref, out_ref, low_ref, high_ref):
    coef = total_of(full_ref, a_ref, b_ref, c_ref)
    for x in range(SLAB):
        value = field_ref[x].astype(F32) - dot(coef, core_ref[x])
        out_ref[x] = value
        short = value.astype(BF16)
        if x < HALO:
            low_ref[x] = short
        if x >= SLAB - HALO:
            high_ref[x - (SLAB - HALO)] = short


def project(full, others, field, core_x):
    rows = field.shape[1]
    return call(
        project_kernel,
        "project",
        (
            struct((SLAB, rows, PLANE), F32),
            struct((HALO, rows, PLANE), BF16),
            struct((HALO, rows, PLANE), BF16),
        ),
        [VMEM] * 6,
    )(full, *others, field, core_x)


UP = [(i, i + 1) for i in range(GRID - 1)]
DOWN = [(j, i) for i, j in UP]


def filter_kernel(inside_ref, field_ref, below_ref, above_ref, weight_ref, core_ref, out_ref, full_ref, half_ref, start, even, odd):
    rows = field_ref.shape[1]
    lane = iota((8, LANES), 1)
    head, tail = lane < 16, lane >= LANES - 16
    first_z, last_z = lane % 16 == 0, lane % 16 == 15
    low_flag, high_flag = inside_ref[0], inside_ref[1]

    def tiles(ref, x, s):
        return [ref[x, s, pl.ds(j * LANES, LANES)] for j in range(TILES)]

    def rolled(mask, value, by):
        return pltpu.roll(jnp.where(mask, 0.0, value), by % LANES, 1)

    def sweep(s):
        source, local = start, s
        for k in range(1, KDEG + 1):
            target = even if k % 2 == 0 else odd
            first, last = k, WIDE - k
            here, after = tiles(source, first - 1, local), tiles(source, first, local)
            for x in range(first, last):
                before, here = here, after
                after = tiles(source, x + 1, local)
                up = [rolled(head, here[j], -16) for j in range(2)]
                down = [rolled(tail, here[j], 16) for j in range(6, 8)]
                for j in range(TILES):
                    lanes = pl.ds(j * LANES, LANES)
                    c = here[j]
                    above_y = here[j + 2] if j < 6 else up[j - 6]
                    below_y = here[j - 2] if j > 1 else down[j]
                    mate = here[j ^ 1]
                    z = mate + (rolled(first_z, mate, -1) if j % 2 else rolled(last_z, mate, 1))
                    around = (before[j] + after[j]) + (above_y + below_y) + z
                    w = jnp.broadcast_to(weight_ref[pl.ds(x, 1), lanes], (8, LANES))
                    value = around - w * c + EK[KDEG - k] * start[x, s, lanes]
                    if x < HALO:
                        value = value * low_flag
                    elif x >= HALO + SLAB:
                        value = value * high_flag
                    if k == KDEG:
                        target[x, :, lanes] = value * TOP
                    else:
                        target[x, :, lanes] = value
            source, local = target, slice(None)

    @pl.loop(0, rows // 16)
    def _(i):
        both = pl.ds(pl.multiple_of(i * 16, 16), 16)
        start[:HALO] = below_ref[:, both, :].astype(F32)
        start[HALO : HALO + SLAB] = field_ref[:, both, :]
        start[HALO + SLAB :] = above_ref[:, both, :].astype(F32)

        @pl.loop(0, 2)
        def _(k):
            sweep(pl.ds(pl.multiple_of(k * 8, 8), 8))
            at = pl.ds(pl.multiple_of(i * 16 + k * 8, 8), 8)
            out_ref[:, at, :] = even[HALO : HALO + SLAB]

    sums(lambda x: out_ref[x].astype(BF16), core_ref, full_ref, half_ref)


def chebyshev(inside, field, below, above, weight, core_x):
    rows = field.shape[1]
    return call(
        filter_kernel,
        "chebyshev",
        (struct((SLAB, rows, PLANE), F32), struct((rows, NCORE), F32), struct((rows, NCORE), BF16)),
        [pl.BlockSpec(memory_space=pltpu.SMEM)] + [VMEM] * 5,
        [
            pltpu.VMEM((WIDE, 16, PLANE), F32),
            pltpu.VMEM((WIDE, 8, PLANE), F32),
            pltpu.VMEM((WIDE, 8, PLANE), F32),
        ],
    )(inside, field, below, above, weight, core_x)


def clean_kernel(full_ref, a_ref, b_ref, c_ref, field_ref, mapped_ref, core_ref, order_ref, own_ref, density_ref, own, sum_rows):
    coef = total_of(full_ref, a_ref, b_ref, c_ref)
    for x in range(SLAB):
        value = field_ref[x] - dot(coef, core_ref[x])
        own[x * BATCH : (x + 1) * BATCH] = value[:BATCH]
        weighted = jnp.sum(mapped_ref[x].astype(F32) * value, axis=0, keepdims=True)
        sum_rows[x : x + 1] = weighted / (3.0 * BATCH)
    back = row_permutation(BATCH * SLAB, BATCH)
    rest, total = own[...], None
    for _ in range(2):
        part = rest.astype(BF16)
        rest = rest - part.astype(F32)
        moved = dot(dot(back, part).astype(BF16), order_ref[...])
        total = moved if total is None else total + moved
    own_ref[...] = total
    rest, total = sum_rows[...], None
    for _ in range(2):
        part = rest.astype(BF16)
        rest = rest - part.astype(F32)
        moved = dot(part, order_ref[...])
        total = moved if total is None else total + moved
    density_ref[...] = total


def clean(full, others, field, mapped, core_x, order):
    return call(
        clean_kernel,
        "clean",
        (struct((SLAB * BATCH, PLANE), F32), struct((SLAB, PLANE), F32)),
        [VMEM] * 8,
        [pltpu.VMEM((SLAB * BATCH, PLANE), F32), pltpu.VMEM((SLAB, PLANE), F32)],
        limit=12,
    )(full, *others, field, mapped, core_x, order)


def shifted(array, by):
    devices = lax.axis_size("group")
    return lax.ppermute(array, "group", [(i, (i + by) % devices) for i in range(devices)])


def body(stochastic, plane_map, core_orbitals, potential):
    local = potential[0]
    below_v = lax.ppermute(local[SLAB - HALO :], "grid", UP)
    above_v = lax.ppermute(local[:HALO], "grid", DOWN)
    place = lax.axis_index("grid")
    inside = jnp.stack([place > 0, place < GRID - 1]).astype(F32)
    stochastic_later, below_v, above_v, inside = lax.optimization_barrier(
        (stochastic, below_v, above_v, inside)
    )
    third = shifted(stochastic_later, 2)
    second = shifted(stochastic_later, 1)

    order, index_row, weight = prepare(plane_map, local, below_v, above_v)
    core_x = relayout(core_orbitals[0])
    mapped, full, half = map_batches(index_row, core_x, (stochastic, second, third))
    field, low, high = project(full, exchange(half), mapped, core_x)
    below = lax.ppermute(high, "grid", UP)
    above = lax.ppermute(low, "grid", DOWN)
    filtered, full, half = chebyshev(inside, field, below, above, weight, core_x)
    own, density = clean(full, exchange(half), filtered, mapped, core_x, order)
    return density[None], own.reshape(BATCH, SLAB, PLANE)


def solution(mesh):
    return jax.shard_map(
        body,
        mesh=mesh,
        in_specs=(
            P("group", "grid", None),
            P("group", None),
            P("group", None, "grid", None),
            P("group", "grid", None),
        ),
        out_specs=(P("group", "grid", None), P("group", "grid", None)),
        check_vma=False,
    )
```

profile of v0, /device:TPU:0, one launch (start us, length us, event | category | flops | bytes accessed | tf_op | source)
XLA Modules:
  0.0 102.9 jit_solution(15311184883493918873)
XLA Ops:
  0.6 0.8 slice_bitcast_fusion
  1.5 1.3 %collective-permute-start.1 = (f32[6,1024]{1,0:T(8,128)S(1)}, f32[6,1024]{1,0:T(8,128)S(1)}, u32[]{:S(2)}, u32[]{:S(2)}) collective-permute-start(f32[6,1024]{1,0:T(8,128)S(1)} %get-tuple-element.38), channel_id=1, source_target_pairs={{1,0},{2,1},{3,2},{5,4},{6,5},{7,6},{9,8},{10,9},{11,10},{13,12},{... | collective-permute-start | bytes 73736 | tf_op jit(solution)/shard_map/ppermute | solution.py:360
  2.8 3.0 %collective-permute-start = (f32[6,1024]{1,0:T(8,128)S(1)}, f32[6,1024]{1,0:T(8,128)S(1)}, u32[]{:S(2)}, u32[]{:S(2)}) collective-permute-start(f32[6,1024]{1,0:T(8,128)S(1)} %get-tuple-element.39), channel_id=1, source_target_pairs={{0,1},{1,2},{2,3},{4,5},{5,6},{6,7},{8,9},{9,10},{10,11},{12,13},{... | collective-permute-start | bytes 73736 | tf_op jit(solution)/shard_map/ppermute | solution.py:359
  5.8 0.1 add_convert_fusion.inside_ref
  5.9 0.0 collective-permute-done.1.above_ref
  5.9 0.8 collective-permute-done.below_ref
  6.6 2.0 %collective-permute-start.3 = (bf16[32,8,1024]{2,1,0:T(8,128)(2,1)}, bf16[32,8,1024]{2,1,0:T(8,128)(2,1)S(1)}, u32[]{:S(2)}, u32[]{:S(2)}) collective-permute-start(bf16[32,8,1024]{2,1,0:T(8,128)(2,1)} %param.4), channel_id=1, source_target_pairs={{0,8},{4,12},{8,16},{12,20},{16,24},{20,28},{24,32},{28,36},{32,40... | collective-permute-start | bytes 1572872 | tf_op jit(solution)/shard_map/ppermute | solution.py:354
  8.7 3.2 %collective-permute-start.2 = (bf16[32,8,1024]{2,1,0:T(8,128)(2,1)}, bf16[32,8,1024]{2,1,0:T(8,128)(2,1)S(1)}, u32[]{:S(2)}, u32[]{:S(2)}) collective-permute-start(bf16[32,8,1024]{2,1,0:T(8,128)(2,1)} %param.4), channel_id=1, source_target_pairs={{0,4},{4,8},{8,12},{12,16},{16,20},{20,24},{24,28},{28,32},{32,36}... | collective-permute-start | bytes 1572872 | tf_op jit(solution)/shard_map/ppermute | solution.py:354
  11.9 0.0 copy-start
  11.9 3.4 %copy-done = bf16[1,512,8,1024]{3,2,1,0:T(8,128)(2,1)S(1)} copy-done((bf16[1,512,8,1024]{3,2,1,0:T(8,128)(2,1)S(1)}, bf16[1,512,8,1024]{3,2,1,0:T(8,128)(2,1)}, u32[]{:S(2)}) %copy-start) | copy-done | bytes 8388632
  15.2 0.0 copy-start.2
  15.2 0.0 copy-start.3
  15.3 0.0 copy-start.1
  15.3 13.5 %relayout.1.refs_1_.core_ref = bf16[8,512,1024]{2,1,0:T(8,128)(2,1)S(1)} custom-call(bf16[4096,1024]{1,0:T(8,128)(2,1)S(1)} %bitcast.13), custom_call_target="tpu_custom_call" | custom-call | tf_op jit(solution)/shard_map/relayout/pallas_call | solution.py:158
  28.7 0.0 copy-done.2
  28.7 0.0 copy-done.3
  28.7 6.0 %prepare.1 = (bf16[1024,1024]{1,0:T(8,128)(2,1)S(1)}, s32[1,1024]{1,0:T(1,128)S(1)}, f32[20,1024]{1,0:T(8,128)S(1)}) custom-call(s32[1,1024]{1,0:T(1,128)S(1)} %copy-done.3, f32[8,1024]{1,0:T(8,128)S(1)} %bitcast.17, f32[6,1024]{1,0:T(8,128)S(1)} %collective-permute-done.below_ref, f32[6,1024]{1,0:T(8,128)S(1)} %collective-permute-done.1.above_ref), custom_call_target="tpu_custom_call" | custom-call | tf_op jit(solution)/shard_map/prepare/pallas_call | solution.py:113
  34.7 0.0 collective-permute-done.3
  34.7 4.5 %collective-permute-done.2 = bf16[32,8,1024]{2,1,0:T(8,128)(2,1)S(1)} collective-permute-done((bf16[32,8,1024]{2,1,0:T(8,128)(2,1)}, bf16[32,8,1024]{2,1,0:T(8,128)(2,1)S(1)}, u32[]{:S(2)}, u32[]{:S(2)}) %collective-permute-start.2) | collective-permute-done | bytes 524320 | tf_op jit(solution)/shard_map/ppermute | solution.py:354
  39.3 0.0 copy-done.1
  39.3 4.8 %map_batches.1 = (bf16[8,96,1024]{2,1,0:T(8,128)(2,1)S(1)}, f32[96,512]{1,0:T(8,128)S(1)}, bf16[96,512]{1,0:T(8,128)(2,1)S(1)}) custom-call(s32[1,1024]{1,0:T(1,128)S(1)} %get-tuple-element.23.refs_0_, bf16[8,512,1024]{2,1,0:T(8,128)(2,1)S(1)} %relayout.1.refs_1_.core_ref, bf16[256,1024]{1,0:T(8,128)(2,1)S(1)} %bitcast.14, bf16[256,1024]{1,0:T(8,128)(2,1)S(1)} %bitcast.16, ...), custom_call_target="tpu_custom_call" | custom-call | tf_op jit(solution)/shard_map/map_batches/pallas_call | solution.py:191
  44.1 0.1 collective-permute-start.6
  44.2 2.0 %collective-permute-start.5 = (bf16[96,512]{1,0:T(8,128)(2,1)S(1)}, bf16[96,512]{1,0:T(8,128)(2,1)S(1)}, u32[]{:S(2)}, u32[]{:S(2)}) collective-permute-start(bf16[96,512]{1,0:T(8,128)(2,1)S(1)} %get-tuple-element.26), channel_id=1, source_target_pairs={{0,2},{1,3},{2,0},{3,1},{4,6},{5,7},{6,4},{7,5},{8,10},{9,11},{10,... | collective-permute-start | bytes 294920 | tf_op jit(solution)/shard_map/ppermute | solution.py:203
  46.2 0.0 collective-permute-start.4
  46.2 2.5 %collective-permute-done.6.c_ref = bf16[96,512]{1,0:T(8,128)(2,1)S(1)} collective-permute-done((bf16[96,512]{1,0:T(8,128)(2,1)S(1)}, bf16[96,512]{1,0:T(8,128)(2,1)S(1)}, u32[]{:S(2)}, u32[]{:S(2)}) %collective-permute-start.6) | collective-permute-done | bytes 98336 | tf_op jit(solution)/shard_map/ppermute | solution.py:203
  48.7 2.7 %collective-permute-done.5.b_ref = bf16[96,512]{1,0:T(8,128)(2,1)S(1)} collective-permute-done((bf16[96,512]{1,0:T(8,128)(2,1)S(1)}, bf16[96,512]{1,0:T(8,128)(2,1)S(1)}, u32[]{:S(2)}, u32[]{:S(2)}) %collective-permute-start.5) | collective-permute-done | bytes 98336 | tf_op jit(solution)/shard_map/ppermute | solution.py:203
  51.4 0.0 collective-permute-done.4.a_ref
  51.4 1.5 %project.1 = (f32[8,96,1024]{2,1,0:T(8,128)S(1)}, bf16[6,96,1024]{2,1,0:T(8,128)(2,1)S(1)}, bf16[6,96,1024]{2,1,0:T(8,128)(2,1)S(1)}) custom-call(f32[96,512]{1,0:T(8,128)S(1)} %get-tuple-element.25.full_ref, bf16[96,512]{1,0:T(8,128)(2,1)S(1)} %collective-permute-done.4.a_ref, bf16[96,512]{1,0:T(8,128)(2,1)S(1)} %collective-permute-done.5.b_ref, ...), custom_call_target="tpu_custom_call" | custom-call | tf_op jit(solution)/shard_map/project/pallas_call | solution.py:226
  52.9 1.5 %collective-permute-start.7 = (bf16[6,96,1024]{2,1,0:T(8,128)(2,1)S(1)}, bf16[6,96,1024]{2,1,0:T(8,128)(2,1)S(1)}, u32[]{:S(2)}, u32[]{:S(2)}) collective-permute-start(bf16[6,96,1024]{2,1,0:T(8,128)(2,1)S(1)} %get-tuple-element.29), channel_id=1, source_target_pairs={{0,1},{1,2},{2,3},{4,5},{5,6},{6,7},{8,9},{9,10},{10,11},{12,13},{... | collective-permute-start | bytes 3538952 | tf_op jit(solution)/shard_map/ppermute | solution.py:373
  54.4 1.5 %collective-permute-start.8 = (bf16[6,96,1024]{2,1,0:T(8,128)(2,1)S(1)}, bf16[6,96,1024]{2,1,0:T(8,128)(2,1)S(1)}, u32[]{:S(2)}, u32[]{:S(2)}) collective-permute-start(bf16[6,96,1024]{2,1,0:T(8,128)(2,1)S(1)} %get-tuple-element.30), channel_id=1, source_target_pairs={{1,0},{2,1},{3,2},{5,4},{6,5},{7,6},{9,8},{10,9},{11,10},{13,12},{... | collective-permute-start | bytes 3538952 | tf_op jit(solution)/shard_map/ppermute | solution.py:374
  55.9 0.9 collective-permute-done.7.below_ref
  56.8 2.8 %collective-permute-done.8.above_ref = bf16[6,96,1024]{2,1,0:T(8,128)(2,1)S(1)} collective-permute-done((bf16[6,96,1024]{2,1,0:T(8,128)(2,1)S(1)}, bf16[6,96,1024]{2,1,0:T(8,128)(2,1)S(1)}, u32[]{:S(2)}, u32[]{:S(2)}) %collective-permute-start.8) | collective-permute-done | bytes 1179680 | tf_op jit(solution)/shard_map/ppermute | solution.py:374
  59.6 19.9 %chebyshev.1 = (f32[8,96,1024]{2,1,0:T(8,128)S(1)}, f32[96,512]{1,0:T(8,128)S(1)}, bf16[96,512]{1,0:T(8,128)(2,1)S(1)}) custom-call(f32[2]{0:T(128)S(1)} %add_convert_fusion.inside_ref, f32[8,96,1024]{2,1,0:T(8,128)S(1)} %get-tuple-element.28.field_ref, bf16[6,96,1024]{2,1,0:T(8,128)(2,1)S(1)} %collective-permute-done.7.below_ref, ...), custom_call_target="tpu_custom_call" | custom-call | tf_op jit(solution)/shard_map/chebyshev/pallas_call | solution.py:304
  79.5 0.3 collective-permute-start.11
  79.8 14.7 %collective-permute-start.10 = (bf16[96,512]{1,0:T(8,128)(2,1)S(1)}, bf16[96,512]{1,0:T(8,128)(2,1)S(1)}, u32[]{:S(2)}, u32[]{:S(2)}) collective-permute-start(bf16[96,512]{1,0:T(8,128)(2,1)S(1)} %get-tuple-element.33), channel_id=1, source_target_pairs={{0,2},{1,3},{2,0},{3,1},{4,6},{5,7},{6,4},{7,5},{8,10},{9,11},{10,... | collective-permute-start | bytes 294920 | tf_op jit(solution)/shard_map/ppermute | solution.py:203
  94.5 0.0 collective-permute-start.9
  94.5 0.0 collective-permute-done.11.c_ref
  94.5 4.2 %collective-permute-done.10.b_ref = bf16[96,512]{1,0:T(8,128)(2,1)S(1)} collective-permute-done((bf16[96,512]{1,0:T(8,128)(2,1)S(1)}, bf16[96,512]{1,0:T(8,128)(2,1)S(1)}, u32[]{:S(2)}, u32[]{:S(2)}) %collective-permute-start.10) | collective-permute-done | bytes 98336 | tf_op jit(solution)/shard_map/ppermute | solution.py:203
  98.7 0.0 collective-permute-done.9.a_ref
  98.7 4.2 %clean.1 = (f32[256,1024]{1,0:T(8,128)}, f32[8,1024]{1,0:T(8,128)}) custom-call(f32[96,512]{1,0:T(8,128)S(1)} %get-tuple-element.32.full_ref, bf16[96,512]{1,0:T(8,128)(2,1)S(1)} %collective-permute-done.9.a_ref, bf16[96,512]{1,0:T(8,128)(2,1)S(1)} %collective-permute-done.10.b_ref, bf16[96,512]{1,0:T(8,128)(2,1)S(1)} %collective-permute-done.11.c_ref, ...), custom_call_target="tpu_custom_call" | custom-call | tf_op jit(solution)/shard_map/clean/pallas_call | solution.py:342
Async XLA Ops:
  1.5 4.4 %collective-permute-start.1 = (f32[6,1024]{1,0:T(8,128)S(1)}, f32[6,1024]{1,0:T(8,128)S(1)}, u32[]{:S(2)}, u32[]{:S(2)}) collective-permute-start(f32[6,1024]{1,0:T(8,128)S(1)} %get-tuple-element.38), channel_id=1, source_target_pairs={{1,0},{2,1},{3,2},{5,4},{6,5},{7,6},{9,8},{10,9},{11,10},{13,12},{... | collective-permute-start | bytes 73736 | tf_op jit(solution)/shard_map/ppermute | solution.py:360
  2.8 3.9 %collective-permute-start = (f32[6,1024]{1,0:T(8,128)S(1)}, f32[6,1024]{1,0:T(8,128)S(1)}, u32[]{:S(2)}, u32[]{:S(2)}) collective-permute-start(f32[6,1024]{1,0:T(8,128)S(1)} %get-tuple-element.39), channel_id=1, source_target_pairs={{0,1},{1,2},{2,3},{4,5},{5,6},{6,7},{8,9},{9,10},{10,11},{12,13},{... | collective-permute-start | bytes 73736 | tf_op jit(solution)/shard_map/ppermute | solution.py:359
  6.6 28.1 %collective-permute-start.3 = (bf16[32,8,1024]{2,1,0:T(8,128)(2,1)}, bf16[32,8,1024]{2,1,0:T(8,128)(2,1)S(1)}, u32[]{:S(2)}, u32[]{:S(2)}) collective-permute-start(bf16[32,8,1024]{2,1,0:T(8,128)(2,1)} %param.4), channel_id=1, source_target_pairs={{0,8},{4,12},{8,16},{12,20},{16,24},{20,28},{24,32},{28,36},{32,40... | collective-permute-start | bytes 1572872 | tf_op jit(solution)/shard_map/ppermute | solution.py:354
  8.7 30.6 %collective-permute-start.2 = (bf16[32,8,1024]{2,1,0:T(8,128)(2,1)}, bf16[32,8,1024]{2,1,0:T(8,128)(2,1)S(1)}, u32[]{:S(2)}, u32[]{:S(2)}) collective-permute-start(bf16[32,8,1024]{2,1,0:T(8,128)(2,1)} %param.4), channel_id=1, source_target_pairs={{0,4},{4,8},{8,12},{12,16},{16,20},{20,24},{24,28},{28,32},{32,36}... | collective-permute-start | bytes 1572872 | tf_op jit(solution)/shard_map/ppermute | solution.py:354
  11.9 3.4 %copy-start = (bf16[1,512,8,1024]{3,2,1,0:T(8,128)(2,1)S(1)}, bf16[1,512,8,1024]{3,2,1,0:T(8,128)(2,1)}, u32[]{:S(2)}) copy-start(bf16[1,512,8,1024]{3,2,1,0:T(8,128)(2,1)} %param.6) | copy-start | bytes 25165828
  15.2 13.5 %copy-start.2 = (f32[1,8,1024]{2,1,0:T(8,128)S(1)}, f32[1,8,1024]{2,1,0:T(8,128)}, u32[]{:S(2)}) copy-start(f32[1,8,1024]{2,1,0:T(8,128)} %param.7) | copy-start | bytes 98308
  15.2 13.5 %copy-start.3 = (s32[1,1024]{1,0:T(1,128)S(1)}, s32[1,1024]{1,0:T(1,128)}, u32[]{:S(2)}) copy-start(s32[1,1024]{1,0:T(1,128)} %index_ref.1) | copy-start | bytes 12292
  15.3 24.0 %copy-start.1 = (bf16[32,8,1024]{2,1,0:T(8,128)(2,1)S(1)}, bf16[32,8,1024]{2,1,0:T(8,128)(2,1)}, u32[]{:S(2)}) copy-start(bf16[32,8,1024]{2,1,0:T(8,128)(2,1)} %param.4) | copy-start | bytes 1572868
  44.1 4.6 %collective-permute-start.6 = (bf16[96,512]{1,0:T(8,128)(2,1)S(1)}, bf16[96,512]{1,0:T(8,128)(2,1)S(1)}, u32[]{:S(2)}, u32[]{:S(2)}) collective-permute-start(bf16[96,512]{1,0:T(8,128)(2,1)S(1)} %get-tuple-element.26), channel_id=1, source_target_pairs={{0,3},{1,2},{2,1},{3,0},{4,7},{5,6},{6,5},{7,4},{8,11},{9,10},{10,... | collective-permute-start | bytes 294920 | tf_op jit(solution)/shard_map/ppermute | solution.py:203
  44.2 7.2 %collective-permute-start.5 = (bf16[96,512]{1,0:T(8,128)(2,1)S(1)}, bf16[96,512]{1,0:T(8,128)(2,1)S(1)}, u32[]{:S(2)}, u32[]{:S(2)}) collective-permute-start(bf16[96,512]{1,0:T(8,128)(2,1)S(1)} %get-tuple-element.26), channel_id=1, source_target_pairs={{0,2},{1,3},{2,0},{3,1},{4,6},{5,7},{6,4},{7,5},{8,10},{9,11},{10,... | collective-permute-start | bytes 294920 | tf_op jit(solution)/shard_map/ppermute | solution.py:203
  46.2 5.2 %collective-permute-start.4 = (bf16[96,512]{1,0:T(8,128)(2,1)S(1)}, bf16[96,512]{1,0:T(8,128)(2,1)S(1)}, u32[]{:S(2)}, u32[]{:S(2)}) collective-permute-start(bf16[96,512]{1,0:T(8,128)(2,1)S(1)} %get-tuple-element.26), channel_id=1, source_target_pairs={{0,1},{1,0},{2,3},{3,2},{4,5},{5,4},{6,7},{7,6},{8,9},{9,8},{10,11... | collective-permute-start | bytes 294920 | tf_op jit(solution)/shard_map/ppermute | solution.py:203
  52.9 3.9 %collective-permute-start.7 = (bf16[6,96,1024]{2,1,0:T(8,128)(2,1)S(1)}, bf16[6,96,1024]{2,1,0:T(8,128)(2,1)S(1)}, u32[]{:S(2)}, u32[]{:S(2)}) collective-permute-start(bf16[6,96,1024]{2,1,0:T(8,128)(2,1)S(1)} %get-tuple-element.29), channel_id=1, source_target_pairs={{0,1},{1,2},{2,3},{4,5},{5,6},{6,7},{8,9},{9,10},{10,11},{12,13},{... | collective-permute-start | bytes 3538952 | tf_op jit(solution)/shard_map/ppermute | solution.py:373
  54.4 5.2 %collective-permute-start.8 = (bf16[6,96,1024]{2,1,0:T(8,128)(2,1)S(1)}, bf16[6,96,1024]{2,1,0:T(8,128)(2,1)S(1)}, u32[]{:S(2)}, u32[]{:S(2)}) collective-permute-start(bf16[6,96,1024]{2,1,0:T(8,128)(2,1)S(1)} %get-tuple-element.30), channel_id=1, source_target_pairs={{1,0},{2,1},{3,2},{5,4},{6,5},{7,6},{9,8},{10,9},{11,10},{13,12},{... | collective-permute-start | bytes 3538952 | tf_op jit(solution)/shard_map/ppermute | solution.py:374
  79.5 15.0 %collective-permute-start.11 = (bf16[96,512]{1,0:T(8,128)(2,1)S(1)}, bf16[96,512]{1,0:T(8,128)(2,1)S(1)}, u32[]{:S(2)}, u32[]{:S(2)}) collective-permute-start(bf16[96,512]{1,0:T(8,128)(2,1)S(1)} %get-tuple-element.33), channel_id=1, source_target_pairs={{0,3},{1,2},{2,1},{3,0},{4,7},{5,6},{6,5},{7,4},{8,11},{9,10},{10,... | collective-permute-start | bytes 294920 | tf_op jit(solution)/shard_map/ppermute | solution.py:203
  79.8 18.9 %collective-permute-start.10 = (bf16[96,512]{1,0:T(8,128)(2,1)S(1)}, bf16[96,512]{1,0:T(8,128)(2,1)S(1)}, u32[]{:S(2)}, u32[]{:S(2)}) collective-permute-start(bf16[96,512]{1,0:T(8,128)(2,1)S(1)} %get-tuple-element.33), channel_id=1, source_target_pairs={{0,2},{1,3},{2,0},{3,1},{4,6},{5,7},{6,4},{7,5},{8,10},{9,11},{10,... | collective-permute-start | bytes 294920 | tf_op jit(solution)/shard_map/ppermute | solution.py:203
  94.5 4.2 %collective-permute-start.9 = (bf16[96,512]{1,0:T(8,128)(2,1)S(1)}, bf16[96,512]{1,0:T(8,128)(2,1)S(1)}, u32[]{:S(2)}, u32[]{:S(2)}) collective-permute-start(bf16[96,512]{1,0:T(8,128)(2,1)S(1)} %get-tuple-element.33), channel_id=1, source_target_pairs={{0,1},{1,0},{2,3},{3,2},{4,5},{5,4},{6,7},{7,6},{8,9},{9,8},{10,11... | collective-permute-start | bytes 294920 | tf_op jit(solution)/shard_map/ppermute | solution.py:203
where the time goes:
time: 103 us
  Pallas kernels  49.8 us (48%)
  starting transfers between devices  29.6 us (29%)
  waiting for transfers between devices  18.5 us (18%)
  local copies, waits for them, and re-layouts  4.23 us (4%)
    pallas_call x1, Pallas kernels, chebyshev(): call(filter_kernel, 'chebyshev', (struct((SLAB, rows, PLANE), F32), struc...  19.9 us
    ppermute x6, starting transfers between devices, exchange(): lax.ppermute(half, 'grid', [(i, i ^ k) for i in range(GRID)])  17.1 us
    pallas_call x1, Pallas kernels, relayout(): call(relayout_kernel, 'relayout', struct((SLAB, NCORE, PLANE), BF16), [VM...  13.5 us
    ppermute x6, waiting for transfers between devices, exchange(): lax.ppermute(half, 'grid', [(i, i ^ k) for i in range(GRID)])  9.41 us
    pallas_call x1, Pallas kernels, prepare(): call(prepare_kernel, 'prepare', (struct((PLANE, PLANE), BF16), struct((1,...  5.97 us
    ppermute x2, starting transfers between devices, shifted(): lax.ppermute(array, 'group', [(i, (i + by) % devices) for i in range(devi...  5.22 us
    pallas_call x1, Pallas kernels, map_batches(): call(map_kernel, 'map_batches', (struct((SLAB, rows, PLANE), BF16), struc...  4.82 us
    ppermute x2, waiting for transfers between devices, shifted(): lax.ppermute(array, 'group', [(i, (i + by) % devices) for i in range(devi...  4.57 us
  transfers between devices with their start and end apart: 12, of which 7 were waited for; matrix products, arithmetic and copies ran while one was open for 0% of the time, Pallas kernels for 19%

commit v1 on v0

v1 whole, which is shorter than its diff:
```python
from fractions import Fraction

import jax
import jax.numpy as jnp
from jax import lax
from jax.experimental import pallas as pl
from jax.experimental.pallas import tpu as pltpu
from jax.sharding import PartitionSpec as P

BZ = 32
KDEG = 6
BATCH = 32
NCORE = 512
SLAB = 8
PLANE = 1024
GRID = 4
HALO = KDEG
WIDE = SLAB + 2 * HALO
LANES = 128
TILES = PLANE // LANES
F32 = jnp.float32
BF16 = jnp.bfloat16


def horner_coefficients():
    cheb = [[Fraction(1)], [Fraction(0), Fraction(1)]]
    for _ in range(2, KDEG + 1):
        last, before = cheb[-1], cheb[-2]
        nxt = [Fraction(0)] + [2 * v for v in last]
        for i, v in enumerate(before):
            nxt[i] -= v
        cheb.append(nxt)
    mono = [Fraction(0)] * (KDEG + 1)
    for k, poly in enumerate(cheb):
        for i, v in enumerate(poly):
            mono[i] += v / (k + 1)
    scaled = [v / Fraction(-8) ** i for i, v in enumerate(mono)]
    top = scaled[KDEG]
    return [float(v / top) for v in scaled], float(top)


EK, TOP = horner_coefficients()

VMEM = pl.BlockSpec(memory_space=pltpu.VMEM)
ANY = pl.BlockSpec(memory_space=pl.ANY)
MIB = 1 << 20
PIECE = 32
CHUNKS = NCORE // PIECE
NT = (((1,), (1,)), ((), ()))


class Line:
    def __init__(self):
        self.token = None

    def call(self, kernel, name, out_shape, args, specs=None, scratch=(), limit=8, micros=2):
        specs = list(specs or [VMEM] * len(args))
        args = list(args)
        waits = self.token is not None
        if waits:
            args.append(self.token)
            specs.append(ANY)
        outs = tuple(out_shape) + (struct((8, LANES), F32),)

        def with_token(*refs):
            ins, rest = refs[: len(args)], refs[len(args) :]
            mine, token, extra = rest[: len(outs) - 1], rest[len(outs) - 1], rest[len(outs) :]
            kernel(*ins[: len(args) - waits], *mine, *extra)
            token[...] = jnp.zeros((8, LANES), F32)

        got = pl.pallas_call(
            with_token,
            in_specs=specs,
            out_specs=tuple(VMEM for _ in outs),
            out_shape=outs,
            scratch_shapes=list(scratch),
            compiler_params=pltpu.CompilerParams(vmem_limit_bytes=limit * MIB),
            cost_estimate=pl.CostEstimate(
                flops=int(micros * 500e6), bytes_accessed=1024, transcendentals=0
            ),
            name=name,
        )(*args)
        self.token = got[-1]
        return got[:-1]


def struct(shape, dtype):
    return jax.ShapeDtypeStruct(shape, dtype)


def one_hot(condition):
    return jnp.where(condition, 1.0, 0.0).astype(BF16)


def iota(shape, axis):
    return lax.broadcasted_iota(jnp.int32, shape, axis)


def dot(a, b):
    return jnp.dot(a, b, preferred_element_type=F32)


def dot_nt(a, b):
    return lax.dot_general(a, b, NT, preferred_element_type=F32)


def split(value, parts):
    out = []
    for _ in range(parts):
        out.append(value.astype(BF16))
        value = value - out[-1].astype(F32)
    return out


def row_permutation(rows, inner):
    outer = rows // inner
    out, src = iota((rows, rows), 0), iota((rows, rows), 1)
    return one_hot(src == (out % outer) * inner + out // outer)


def natural_point(q):
    tile, lane = q // LANES, q % LANES
    return (4 * (lane // 16) + tile // 2) * BZ + 2 * (lane % 16) + tile % 2


def prepare_kernel(index_ref, local_ref, order_ref, pick_ref, local_out):
    order_ref[...] = one_hot(iota((PLANE, PLANE), 1) == natural_point(iota((PLANE, PLANE), 0)))
    index = index_ref[...]
    digits = jnp.concatenate([index // 32, index % 32] + [jnp.zeros((6, PLANE), jnp.int32)], axis=0)
    rows = jnp.concatenate([digits.astype(F32)] + [p.astype(F32) for p in split(local_ref[...], 3)], axis=0)
    moved = dot_nt(rows.astype(BF16), order_ref[...])
    local_out[...] = (moved[8:16] + moved[16:24]) + moved[24:32]
    index = (moved[0:1] * 32.0 + moved[1:2]).astype(jnp.int32)
    pick_ref[...] = one_hot(iota((PLANE, PLANE), 0) == index)


def prepare(line, plane_map, local):
    square = struct((PLANE, PLANE), BF16)
    return line.call(
        prepare_kernel,
        "prepare",
        (square, square, struct((SLAB, PLANE), F32)),
        (plane_map, local),
        micros=2,
    )


def relayout_kernel(core_hbm, out_ref, raw, mids, rows_ref, columns_ref, sems):
    def fetch(i):
        return pltpu.make_async_copy(core_hbm.at[pl.ds(i * 256, 256), :], raw.at[i], sems.at[i])

    for i in range(CHUNKS):
        fetch(i).start()
    rows_ref[...] = row_permutation(256, SLAB)
    src, out = iota((256, 256), 0), iota((256, 256), 1)
    piece, low = out // PIECE, out % PIECE
    columns_ref[...] = one_hot(src == (4 * (low // 16) + piece // 2) * BZ + 2 * (low % 16) + piece % 2)
    lane = iota((PIECE, LANES), 1)
    half, quarter = lane < 64, lane % 64 < 32

    def permute(i, mid):
        for b in range(4):
            cols = pl.ds(b * 256, 256)
            ordered = dot(rows_ref[...], raw[i, :, cols]).astype(BF16)
            mid[:, cols] = dot(ordered, columns_ref[...]).astype(BF16)

    def gather(i, mid):
        at = pl.ds(pl.multiple_of(i * PIECE, PIECE), PIECE)
        for x in range(SLAB):
            for h in range(2):
                p = [
                    mid[pl.ds(x * PIECE, PIECE), pl.ds(b * 256 + h * LANES, LANES)]
                    for b in range(4)
                ]
                u = [jnp.where(half, p[k], pltpu.roll(p[k + 2], 64, 1)) for k in range(2)]
                v = [jnp.where(half, pltpu.roll(p[k], 64, 1), p[k + 2]) for k in range(2)]
                for k, (a, c) in enumerate((u, v)):
                    j = 4 * h + 2 * k
                    out_ref[x, at, pl.ds(j * LANES, LANES)] = jnp.where(
                        quarter, a, pltpu.roll(c, 32, 1)
                    )
                    out_ref[x, at, pl.ds((j + 1) * LANES, LANES)] = jnp.where(
                        quarter, pltpu.roll(a, LANES - 32, 1), c
                    )

    @pl.loop(0, CHUNKS // 4)
    def _(i):
        for k in range(4):
            fetch(4 * i + k).wait()
        for k in range(5):
            if k < 4:
                permute(4 * i + k, mids.at[k])
            if k > 0:
                gather(4 * i + k - 1, mids.at[k - 1])


def relayout(line, core):
    square = pltpu.VMEM((256, 256), BF16)
    return line.call(
        relayout_kernel,
        "relayout",
        (struct((SLAB, NCORE, PLANE), BF16),),
        (core.reshape(NCORE * SLAB, PLANE),),
        specs=[pl.BlockSpec(memory_space=pltpu.HBM)],
        scratch=[
            pltpu.VMEM((CHUNKS, 256, PLANE), BF16),
            pltpu.VMEM((4, 256, PLANE), BF16),
            square,
            square,
            pltpu.SemaphoreType.DMA((CHUNKS,)),
        ],
        limit=42,
        micros=8,
    )[0]


def sums(field_of, core_ref, full_ref, half_ref):
    for x in range(SLAB):
        part = dot_nt(field_of(x), core_ref[x])
        if x == 0:
            full_ref[...] = part
        else:
            full_ref[...] += part
    half_ref[...] = full_ref[...].astype(BF16)


def map_kernel(counts, pick_ref, core_ref, *refs):
    sources, (out_ref, full_ref, half_ref) = refs[:-3], refs[-3:]
    perm = row_permutation(BATCH * SLAB, SLAB)
    for b, count in enumerate(counts):
        value = sources[0][...]
        if count == 2:
            value = value + sources[1][...]
        sources = sources[count:]
        got = dot(dot(perm, value).astype(BF16), pick_ref[...]).astype(BF16)
        out_ref[:, b * BATCH : (b + 1) * BATCH, :] = got.reshape(SLAB, BATCH, PLANE)
    sums(lambda x: out_ref[x], core_ref, full_ref, half_ref)


def map_batches(line, pick, core_x, batches):
    rows = BATCH * len(batches)
    counts = tuple(len(b) for b in batches)
    flat = [a.reshape(BATCH * SLAB, PLANE) for b in batches for a in b]
    return line.call(
        lambda *refs: map_kernel(counts, *refs),
        "map_batches",
        (struct((SLAB, rows, PLANE), BF16), struct((rows, NCORE), F32), struct((rows, NCORE), BF16)),
        (pick, core_x, *flat),
        micros=2 + len(batches) // 2,
    )


def exchange(half):
    return [
        lax.ppermute(half, "grid", [(i, i ^ k) for i in range(GRID)]) for k in range(1, GRID)
    ]


def total_of(full_ref, a_ref, b_ref, c_ref):
    rest = a_ref[...].astype(F32) + b_ref[...].astype(F32) + c_ref[...].astype(F32)
    return (full_ref[...] + rest).astype(BF16)


def project_kernel(full_ref, a_ref, b_ref, c_ref, field_ref, core_ref, *refs):
    local_ref = refs[0] if len(refs) == 4 else None
    out_ref, low_ref, high_ref = refs[-3:]
    rows = field_ref.shape[1]
    coef = total_of(full_ref, a_ref, b_ref, c_ref)
    for x in range(SLAB):
        value = field_ref[x].astype(F32) - dot(coef, core_ref[x])
        out_ref[x] = value
        short = value.astype(BF16)
        if local_ref is not None:
            parts = [p.astype(F32) for p in split(local_ref[x : x + 1], 3)]
            rest = jnp.zeros((12, PLANE), F32)
            extra = jnp.concatenate(parts + [jnp.ones((1, PLANE), F32), rest], axis=0)
            short = jnp.concatenate([short, extra.astype(BF16)], axis=0)
        if x < HALO:
            low_ref[x] = short
        if x >= SLAB - HALO:
            high_ref[x - (SLAB - HALO)] = short


def project(line, full, others, field, core_x, local):
    rows = field.shape[1]
    sent = rows + (16 if local is not None else 0)
    return line.call(
        project_kernel,
        "project",
        (
            struct((SLAB, rows, PLANE), F32),
            struct((HALO, sent, PLANE), BF16),
            struct((HALO, sent, PLANE), BF16),
        ),
        (full, *others, field, core_x) + ((local,) if local is not None else ()),
        micros=2,
    )


UP = [(i, i + 1) for i in range(GRID - 1)]
DOWN = [(j, i) for i, j in UP]


def filter_kernel(given, *refs):
    field_ref, below_ref, above_ref, core_ref = refs[:4]
    if given:
        weight_ref, flag_ref, out_ref, full_ref, half_ref = refs[4:9]
    else:
        local_ref, weight_ref, flag_ref, out_ref, full_ref, half_ref = refs[4:10]
    below, above, even, odd = refs[-4:]
    rows = field_ref.shape[1]
    if not given:
        weight_ref[HALO : HALO + SLAB] = 8.0 * local_ref[...] - 2.0
        for k, ref in enumerate((below_ref, above_ref)):
            for x in range(HALO):
                extra = ref[x, rows : rows + 16, :].astype(F32)
                near = (extra[0:1] + extra[1:2]) + extra[2:3]
                place = x if k == 0 else HALO + SLAB + x
                weight_ref[place : place + 1] = 8.0 * near - 2.0
                if x == 0:
                    flag_ref[k] = jnp.broadcast_to(extra[3:4, :LANES], (8, LANES))
    lane = iota((8, LANES), 1)
    head, tail = lane < 16, lane >= LANES - 16
    first_z, last_z = lane % 16 == 0, lane % 16 == 15
    low_flag, high_flag = flag_ref[0], flag_ref[1]

    def rolled(mask, value, by):
        return pltpu.roll(jnp.where(mask, 0.0, value), by % LANES, 1)

    def sweep(local, at):
        def begin(x, lanes):
            if x < HALO:
                return below[x, local, lanes]
            if x >= HALO + SLAB:
                return above[x - HALO - SLAB, local, lanes]
            return field_ref[x - HALO, at, lanes]

        def tiles(source, x):
            every = [pl.ds(j * LANES, LANES) for j in range(TILES)]
            if source is None:
                return [begin(x, lanes) for lanes in every]
            return [source[x, :, lanes] for lanes in every]

        source = None
        for k in range(1, KDEG + 1):
            target = even if k % 2 == 0 else odd
            first, last = k, WIDE - k
            here, after = tiles(source, first - 1), tiles(source, first)
            for x in range(first, last):
                before, here = here, after
                after = tiles(source, x + 1)
                up = [rolled(head, here[j], -16) for j in range(2)]
                down = [rolled(tail, here[j], 16) for j in range(6, 8)]
                for j in range(TILES):
                    lanes = pl.ds(j * LANES, LANES)
                    c = here[j]
                    above_y = here[j + 2] if j < 6 else up[j - 6]
                    below_y = here[j - 2] if j > 1 else down[j]
                    mate = here[j ^ 1]
                    z = mate + (rolled(first_z, mate, -1) if j % 2 else rolled(last_z, mate, 1))
                    around = (before[j] + after[j]) + (above_y + below_y) + z
                    w = jnp.broadcast_to(weight_ref[pl.ds(x, 1), lanes], (8, LANES))
                    value = around - w * c + EK[KDEG - k] * begin(x, lanes)
                    if x == HALO - 1:
                        value = value * low_flag
                    elif x == HALO + SLAB:
                        value = value * high_flag
                    if k == KDEG:
                        out_ref[x - HALO, at, lanes] = value * TOP
                    else:
                        target[x, :, lanes] = value
            source = target

    @pl.loop(0, rows // 16)
    def _(i):
        both = pl.ds(pl.multiple_of(i * 16, 16), 16)
        below[...] = below_ref[:, both, :].astype(F32)
        above[...] = above_ref[:, both, :].astype(F32)

        @pl.loop(0, 2)
        def _(k):
            sweep(
                pl.ds(pl.multiple_of(k * 8, 8), 8),
                pl.ds(pl.multiple_of(i * 16 + k * 8, 8), 8),
            )

    sums(lambda x: out_ref[x].astype(BF16), core_ref, full_ref, half_ref)


def chebyshev(line, field, below, above, core_x, local, weight):
    rows = field.shape[1]
    made = (struct((WIDE, PLANE), F32), struct((2, 8, LANES), F32))
    given = weight is not None
    got = line.call(
        lambda *refs: filter_kernel(given, *refs),
        "chebyshev",
        (() if given else made)
        + (struct((SLAB, rows, PLANE), F32), struct((rows, NCORE), F32), struct((rows, NCORE), BF16)),
        (field, below, above, core_x) + (tuple(weight) if given else (local,)),
        scratch=[
            pltpu.VMEM((HALO, 16, PLANE), F32),
            pltpu.VMEM((HALO, 16, PLANE), F32),
            pltpu.VMEM((WIDE, 8, PLANE), F32),
            pltpu.VMEM((WIDE, 8, PLANE), F32),
        ],
        micros=2 + rows // 5,
    )
    return (weight, got) if given else (got[:2], got[2:])


def reorder(value, order_ref):
    parts = split(value, 2)
    return dot(parts[0], order_ref[...]) + dot(parts[1], order_ref[...])


def clean_kernel(first, last, *refs):
    refs = list(refs)
    full_ref, a_ref, b_ref, c_ref, field_ref, mapped_ref, core_ref = refs[:7]
    refs = refs[7:]
    order_ref = refs.pop(0) if first or last else None
    before_ref = None if first else refs.pop(0)
    own_ref = refs.pop(0) if first else None
    density_ref = refs.pop(0)
    own = refs.pop(0) if first else None
    rows = refs.pop(0)
    coef = total_of(full_ref, a_ref, b_ref, c_ref)
    for x in range(SLAB):
        value = field_ref[x] - dot(coef, core_ref[x])
        if first:
            own[x * BATCH : (x + 1) * BATCH] = value[:BATCH]
        weighted = jnp.sum(mapped_ref[x].astype(F32) * value, axis=0, keepdims=True)
        rows[x : x + 1] = weighted / (3.0 * BATCH)
    if first:
        back = row_permutation(BATCH * SLAB, BATCH)
        total = None
        for part in split(own[...], 2):
            moved = dot(dot(back, part).astype(BF16), order_ref[...])
            total = moved if total is None else total + moved
        own_ref[...] = total
    density = rows[...] if first else rows[...] + before_ref[...]
    density_ref[...] = reorder(density, order_ref) if last else density


def clean(line, full, others, field, mapped, core_x, order, density, first, last):
    args = [full, *others, field, mapped, core_x]
    if first or last:
        args.append(order)
    if not first:
        args.append(density)
    small = struct((SLAB, PLANE), F32)
    own = struct((SLAB * BATCH, PLANE), F32)
    got = line.call(
        lambda *refs: clean_kernel(first, last, *refs),
        "clean",
        (own, small) if first else (small,),
        args,
        scratch=([pltpu.VMEM(own.shape, F32)] if first else []) + [pltpu.VMEM(small.shape, F32)],
        limit=12,
        micros=3,
    )
    return (got[0], got[1]) if first else (None, got[0])


def permute_groups(array, pairs):
    return lax.ppermute(array, "group", pairs)


def body(stochastic, plane_map, core_orbitals, potential):
    groups = lax.axis_size("group")
    third = permute_groups(stochastic, [(i, (i + 2) % groups) for i in range(groups)])
    to_odd = permute_groups(stochastic, [(i, i + 1) for i in range(0, groups, 2)])
    to_even = None

    line = Line()
    core_x = relayout(line, core_orbitals[0])
    order, pick, local = prepare(line, plane_map, potential[0])
    state = {}
    weight = density = own = None
    for step, c in PLAN:
        s = state.setdefault(c, {})
        if step == "forward":
            third, line.token = lax.optimization_barrier((third, line.token))
            to_even = permute_groups(third, [(i + 1, i) for i in range(0, groups, 2)])
        elif step == "map":
            batches = [(stochastic,), (to_odd, to_even), (third,)]
            visits = [batches[t] for t in VISITS[c]]
            s["mapped"], s["full"], half = map_batches(line, pick, core_x, visits)
            s["others"] = exchange(half)
        elif step == "project":
            s["field"], low, high = project(
                line, s["full"], s["others"], s["mapped"], core_x, local if c == 0 else None
            )
            s["below"] = lax.ppermute(high, "grid", UP)
            s["above"] = lax.ppermute(low, "grid", DOWN)
        elif step == "filter":
            weight, (s["done"], s["full"], half) = chebyshev(
                line, s["field"], s["below"], s["above"], core_x, local, weight
            )
            s["others"] = exchange(half)
        elif step == "clean":
            got, density = clean(
                line, s["full"], s["others"], s["done"], s["mapped"], core_x, order, density,
                c == 0, c == len(VISITS) - 1,
            )
            own = got if c == 0 else own
    return density[None], own.reshape(BATCH, SLAB, PLANE)


VISITS = ((0,), (2, 1))
PLAN = (
    ("map", 0),
    ("forward", 0),
    ("project", 0),
    ("map", 1),
    ("project", 1),
    ("filter", 0),
    ("filter", 1),
    ("clean", 0),
    ("clean", 1),
)


def solution(mesh):
    return jax.shard_map(
        body,
        mesh=mesh,
        in_specs=(
            P("group", "grid", None),
            P("group", None),
            P("group", None, "grid", None),
            P("group", "grid", None),
        ),
        out_specs=(P("group", "grid", None), P("group", "grid", None)),
        check_vma=False,
    )
```

time: 103 us -> 97.9 us (0.950)
  the two profiles are of different devices: /device:TPU:0 before, /device:TPU:23 now
where the time goes in v1:
time: 97.9 us; the launch traced here: 97.7 us
  Pallas kernels  51.2 us (52%)
  starting transfers between devices  28.6 us (29%)
  waiting for transfers between devices  17.1 us (17%)
    pallas_call x10, Pallas kernels, call(): pl.pallas_call(with_token, in_specs=specs, out_specs=tuple((VMEM for _ in...  51.2 us
    ppermute x12, waiting for transfers between devices, exchange(): lax.ppermute(half, 'grid', [(i, i ^ k) for i in range(GRID)])  17 us
    ppermute x12, starting transfers between devices, exchange(): lax.ppermute(half, 'grid', [(i, i ^ k) for i in range(GRID)])  9.93 us
    ppermute x3, starting transfers between devices, permute_groups(): return lax.ppermute(array, 'group', pairs)  8.55 us
    ppermute x2, starting transfers between devices, body(): s['below'] = lax.ppermute(high, 'grid', UP)  6.24 us
    ppermute x2, starting transfers between devices, body(): s['above'] = lax.ppermute(low, 'grid', DOWN)  3.84 us
  transfers between devices with their start and end apart: 19, of which 4 were waited for; matrix products, arithmetic and copies ran while one was open for 0% of the time, Pallas kernels for 49%

profile of v1, /device:TPU:23, one launch (start us, length us, event | category | flops | bytes accessed | tf_op | source)
XLA Modules:
  0.0 97.7 jit_solution(17008928606929233468)
XLA Ops:
  0.6 1.7 %collective-permute-start = (bf16[32,8,1024]{2,1,0:T(8,128)(2,1)}, bf16[32,8,1024]{2,1,0:T(8,128)(2,1)S(1)}, u32[]{:S(2)}, u32[]{:S(2)}) collective-permute-start(bf16[32,8,1024]{2,1,0:T(8,128)(2,1)} %param.4), channel_id=1, source_target_pairs={{0,8},{4,12},{8,16},{12,20},{16,24},{20,28},{24,32},{28,36},{32,40... | collective-permute-start | bytes 1572872 | tf_op jit(solution)/shard_map/ppermute | solution.py:465
  2.3 1.3 %collective-permute-start.1 = (bf16[32,8,1024]{2,1,0:T(8,128)(2,1)}, bf16[32,8,1024]{2,1,0:T(8,128)(2,1)S(1)}, u32[]{:S(2)}, u32[]{:S(2)}) collective-permute-start(bf16[32,8,1024]{2,1,0:T(8,128)(2,1)} %param.4), channel_id=1, source_target_pairs={{0,4},{8,12},{16,20},{24,28},{32,36},{40,44},{48,52},{56,60},{64,6... | collective-permute-start | bytes 1572872 | tf_op jit(solution)/shard_map/ppermute | solution.py:465
  3.6 0.0 copy-start.1
  3.6 0.0 copy-start.2
  3.6 8.6 %relayout.1 = (bf16[8,512,1024]{2,1,0:T(8,128)(2,1)S(1)}, f32[8,128]{1,0:T(8,128)S(1)}) custom-call(bf16[4096,1024]{1,0:T(8,128)(2,1)} %bitcast.13), custom_call_target="tpu_custom_call" | custom-call | flops 4000000000 | bytes 1024 | tf_op jit(solution)/shard_map/relayout/pallas_call | solution.py:71
  12.3 0.0 copy-start
  12.3 0.0 copy-done.1
  12.3 0.0 copy-done.2
  12.3 1.8 %prepare.1 = (bf16[1024,1024]{1,0:T(8,128)(2,1)S(1)}, bf16[1024,1024]{1,0:T(8,128)(2,1)S(1)}, f32[8,1024]{1,0:T(8,128)S(1)}, f32[8,128]{1,0:T(8,128)S(1)}) custom-call(s32[1,1024]{1,0:T(1,128)S(1)} %copy-done.2, f32[8,1024]{1,0:T(8,128)S(1)} %bitcast.12, f32[8,128]{1,0:T(8,128)S(1)} %get-tuple-element.40.refs_2_), custom_call_target="tpu_custom_call" | custom-call | flops 1000000000 | bytes 1024 | tf_op jit(solution)/shard_map/prepare/pallas_call | solution.py:71
  14.1 0.0 copy-done
  14.2 3.2 %map_batches.2 = (bf16[8,32,1024]{2,1,0:T(8,128)(2,1)S(1)}, f32[32,512]{1,0:T(8,128)S(1)}, bf16[32,512]{1,0:T(8,128)(2,1)S(1)}, f32[8,128]{1,0:T(8,128)S(1)}) custom-call(bf16[1024,1024]{1,0:T(8,128)(2,1)S(1)} %get-tuple-element.41.refs_0_, bf16[8,512,1024]{2,1,0:T(8,128)(2,1)S(1)} %get-tuple-element.42.refs_1_.refs_5_.refs_3_.refs_6_, ...), custom_call_target="tpu_custom_call" | custom-call | flops 1000000000 | bytes 1024 | tf_op jit(solution)/shard_map/map_batches/pallas_call | solution.py:71
  17.4 0.0 collective-permute-done
  17.4 5.6 %collective-permute-start.2 = (bf16[32,8,1024]{2,1,0:T(8,128)(2,1)S(1)}, bf16[32,8,1024]{2,1,0:T(8,128)(2,1)S(1)}, u32[]{:S(2)}, u32[]{:S(2)}) collective-permute-start(bf16[32,8,1024]{2,1,0:T(8,128)(2,1)S(1)} %collective-permute-done), channel_id=1, source_target_pairs={{4,0},{12,8},{20,16},{28,24},{36,32},{44,40},{52,48},{60,56},{68,6... | collective-permute-start | bytes 1572872 | tf_op jit(solution)/shard_map/ppermute | solution.py:465
  23.0 1.6 %collective-permute-start.3 = (bf16[32,512]{1,0:T(8,128)(2,1)S(1)}, bf16[32,512]{1,0:T(8,128)(2,1)S(1)}, u32[]{:S(2)}, u32[]{:S(2)}) collective-permute-start(bf16[32,512]{1,0:T(8,128)(2,1)S(1)} %get-tuple-element.47), channel_id=1, source_target_pairs={{0,1},{1,0},{2,3},{3,2},{4,5},{5,4},{6,7},{7,6},{8,9},{9,8},{10,11... | collective-permute-start | bytes 98312 | tf_op jit(solution)/shard_map/ppermute | solution.py:255
  24.6 1.0 %collective-permute-start.4 = (bf16[32,512]{1,0:T(8,128)(2,1)S(1)}, bf16[32,512]{1,0:T(8,128)(2,1)S(1)}, u32[]{:S(2)}, u32[]{:S(2)}) collective-permute-start(bf16[32,512]{1,0:T(8,128)(2,1)S(1)} %get-tuple-element.47), channel_id=1, source_target_pairs={{0,2},{1,3},{2,0},{3,1},{4,6},{5,7},{6,4},{7,5},{8,10},{9,11},{10,... | collective-permute-start | bytes 98312 | tf_op jit(solution)/shard_map/ppermute | solution.py:255
  25.6 0.7 collective-permute-start.5
  26.3 0.0 collective-permute-done.3.refs_1_
  26.3 8.8 %collective-permute-done.4.refs_2_ = bf16[32,512]{1,0:T(8,128)(2,1)S(1)} collective-permute-done((bf16[32,512]{1,0:T(8,128)(2,1)S(1)}, bf16[32,512]{1,0:T(8,128)(2,1)S(1)}, u32[]{:S(2)}, u32[]{:S(2)}) %collective-permute-start.4) | collective-permute-done | bytes 32800 | tf_op jit(solution)/shard_map/ppermute | solution.py:255
  35.1 2.4 %collective-permute-done.5.refs_3_ = bf16[32,512]{1,0:T(8,128)(2,1)S(1)} collective-permute-done((bf16[32,512]{1,0:T(8,128)(2,1)S(1)}, bf16[32,512]{1,0:T(8,128)(2,1)S(1)}, u32[]{:S(2)}, u32[]{:S(2)}) %collective-permute-start.5) | collective-permute-done | bytes 32800 | tf_op jit(solution)/shard_map/ppermute | solution.py:255
  37.5 1.6 %project.2 = (f32[8,32,1024]{2,1,0:T(8,128)S(1)}, bf16[6,48,1024]{2,1,0:T(8,128)(2,1)S(1)}, bf16[6,48,1024]{2,1,0:T(8,128)(2,1)S(1)}, f32[8,128]{1,0:T(8,128)S(1)}) custom-call(f32[32,512]{1,0:T(8,128)S(1)} %get-tuple-element.46.refs_0_, bf16[32,512]{1,0:T(8,128)(2,1)S(1)} %collective-permute-done.3.refs_1_, ...), custom_call_target="tpu_custom_call" | custom-call | flops 1000000000 | bytes 1024 | tf_op jit(solution)/shard_map/project/pallas_call | solution.py:71
  39.1 2.6 %collective-permute-start.11 = (bf16[6,48,1024]{2,1,0:T(8,128)(2,1)S(1)}, bf16[6,48,1024]{2,1,0:T(8,128)(2,1)S(1)}, u32[]{:S(2)}, u32[]{:S(2)}) collective-permute-start(bf16[6,48,1024]{2,1,0:T(8,128)(2,1)S(1)} %get-tuple-element.60), channel_id=1, source_target_pairs={{0,1},{1,2},{2,3},{4,5},{5,6},{6,7},{8,9},{9,10},{10,11},{12,13},{... | collective-permute-start | bytes 1769480 | tf_op jit(solution)/shard_map/ppermute | solution.py:493
  41.7 1.9 %collective-permute-start.12 = (bf16[6,48,1024]{2,1,0:T(8,128)(2,1)S(1)}, bf16[6,48,1024]{2,1,0:T(8,128)(2,1)S(1)}, u32[]{:S(2)}, u32[]{:S(2)}) collective-permute-start(bf16[6,48,1024]{2,1,0:T(8,128)(2,1)S(1)} %get-tuple-element.61), channel_id=1, source_target_pairs={{1,0},{2,1},{3,2},{5,4},{6,5},{7,6},{9,8},{10,9},{11,10},{13,12},{... | collective-permute-start | bytes 1769480 | tf_op jit(solution)/shard_map/ppermute | solution.py:494
  43.6 0.0 collective-permute-done.1
  43.7 0.0 collective-permute-done.2
  43.7 4.1 %map_batches.3 = (bf16[8,64,1024]{2,1,0:T(8,128)(2,1)S(1)}, f32[64,512]{1,0:T(8,128)S(1)}, bf16[64,512]{1,0:T(8,128)(2,1)S(1)}, f32[8,128]{1,0:T(8,128)S(1)}) custom-call(bf16[1024,1024]{1,0:T(8,128)(2,1)S(1)} %get-tuple-element.41.refs_0_, bf16[8,512,1024]{2,1,0:T(8,128)(2,1)S(1)} %get-tuple-element.42.refs_1_.refs_5_.refs_3_.refs_6_, ...), custom_call_target="tpu_custom_call" | custom-call | flops 1500000000 | bytes 1024 | tf_op jit(solution)/shard_map/map_batches/pallas_call | solution.py:71
  47.7 0.1 collective-permute-start.6
  47.8 1.8 %collective-permute-start.7 = (bf16[64,512]{1,0:T(8,128)(2,1)S(1)}, bf16[64,512]{1,0:T(8,128)(2,1)S(1)}, u32[]{:S(2)}, u32[]{:S(2)}) collective-permute-start(bf16[64,512]{1,0:T(8,128)(2,1)S(1)} %get-tuple-element.53), channel_id=1, source_target_pairs={{0,2},{1,3},{2,0},{3,1},{4,6},{5,7},{6,4},{7,5},{8,10},{9,11},{10,... | collective-permute-start | bytes 196616 | tf_op jit(solution)/shard_map/ppermute | solution.py:255
  49.6 0.3 collective-permute-start.8
  49.9 0.0 collective-permute-done.6.refs_1_
  49.9 2.1 %collective-permute-done.7.refs_2_ = bf16[64,512]{1,0:T(8,128)(2,1)S(1)} collective-permute-done((bf16[64,512]{1,0:T(8,128)(2,1)S(1)}, bf16[64,512]{1,0:T(8,128)(2,1)S(1)}, u32[]{:S(2)}, u32[]{:S(2)}) %collective-permute-start.7) | collective-permute-done | bytes 65568 | tf_op jit(solution)/shard_map/ppermute | solution.py:255
  52.0 3.7 %collective-permute-done.8.refs_3_ = bf16[64,512]{1,0:T(8,128)(2,1)S(1)} collective-permute-done((bf16[64,512]{1,0:T(8,128)(2,1)S(1)}, bf16[64,512]{1,0:T(8,128)(2,1)S(1)}, u32[]{:S(2)}, u32[]{:S(2)}) %collective-permute-start.8) | collective-permute-done | bytes 65568 | tf_op jit(solution)/shard_map/ppermute | solution.py:255
  55.7 1.6 %project.3 = (f32[8,64,1024]{2,1,0:T(8,128)S(1)}, bf16[6,64,1024]{2,1,0:T(8,128)(2,1)S(1)}, bf16[6,64,1024]{2,1,0:T(8,128)(2,1)S(1)}, f32[8,128]{1,0:T(8,128)S(1)}) custom-call(f32[64,512]{1,0:T(8,128)S(1)} %get-tuple-element.52.refs_0_, bf16[64,512]{1,0:T(8,128)(2,1)S(1)} %collective-permute-done.6.refs_1_, ...), custom_call_target="tpu_custom_call" | custom-call | flops 1000000000 | bytes 1024 | tf_op jit(solution)/shard_map/project/pallas_call | solution.py:71
  57.3 1.9 %collective-permute-start.10 = (bf16[6,64,1024]{2,1,0:T(8,128)(2,1)S(1)}, bf16[6,64,1024]{2,1,0:T(8,128)(2,1)S(1)}, u32[]{:S(2)}, u32[]{:S(2)}) collective-permute-start(bf16[6,64,1024]{2,1,0:T(8,128)(2,1)S(1)} %get-tuple-element.58), channel_id=1, source_target_pairs={{1,0},{2,1},{3,2},{5,4},{6,5},{7,6},{9,8},{10,9},{11,10},{13,12},{... | collective-permute-start | bytes 2359304 | tf_op jit(solution)/shard_map/ppermute | solution.py:494
  59.3 3.6 %collective-permute-start.9 = (bf16[6,64,1024]{2,1,0:T(8,128)(2,1)S(1)}, bf16[6,64,1024]{2,1,0:T(8,128)(2,1)S(1)}, u32[]{:S(2)}, u32[]{:S(2)}) collective-permute-start(bf16[6,64,1024]{2,1,0:T(8,128)(2,1)S(1)} %get-tuple-element.57), channel_id=1, source_target_pairs={{0,1},{1,2},{2,3},{4,5},{5,6},{6,7},{8,9},{9,10},{10,11},{12,13},{... | collective-permute-start | bytes 2359304 | tf_op jit(solution)/shard_map/ppermute | solution.py:493
  62.9 0.0 collective-permute-done.11.refs_1_
  62.9 0.0 collective-permute-done.12.refs_2_
  62.9 8.9 %chebyshev.2 = (f32[20,1024]{1,0:T(8,128)S(1)}, f32[2,8,128]{2,1,0:T(8,128)S(1)}, f32[8,32,1024]{2,1,0:T(8,128)S(1)}, f32[32,512]{1,0:T(8,128)S(1)}, bf16[32,512]{1,0:T(8,128)(2,1)S(1)}, /*index=5*/f32[8,128]{1,0:T(8,128)S(1)}) custom-call(f32[8,32,1024]{2,1,0:T(8,128)S(1)} %get-tuple-element.59.refs_0_, ...), custom_call_target="tpu_custom_call" | custom-call | flops 4000000000 | bytes 1024 | tf_op jit(solution)/shard_map/chebyshev/pallas_call | solution.py:71
  71.9 0.1 collective-permute-start.16
  71.9 0.1 collective-permute-start.17
  72.0 2.0 %collective-permute-start.18 = (bf16[32,512]{1,0:T(8,128)(2,1)S(1)}, bf16[32,512]{1,0:T(8,128)(2,1)S(1)}, u32[]{:S(2)}, u32[]{:S(2)}) collective-permute-start(bf16[32,512]{1,0:T(8,128)(2,1)S(1)} %get-tuple-element.71), channel_id=1, source_target_pairs={{0,3},{1,2},{2,1},{3,0},{4,7},{5,6},{6,5},{7,4},{8,11},{9,10},{10,... | collective-permute-start | bytes 98312 | tf_op jit(solution)/shard_map/ppermute | solution.py:255
  74.1 0.0 collective-permute-done.10.refs_2_
  74.1 0.0 collective-permute-done.9.refs_1_
  74.1 14.4 %chebyshev.3 = (f32[8,64,1024]{2,1,0:T(8,128)S(1)}, f32[64,512]{1,0:T(8,128)S(1)}, bf16[64,512]{1,0:T(8,128)(2,1)S(1)}, f32[8,128]{1,0:T(8,128)S(1)}) custom-call(f32[8,64,1024]{2,1,0:T(8,128)S(1)} %get-tuple-element.56.refs_0_, bf16[6,64,1024]{2,1,0:T(8,128)(2,1)S(1)} %collective-permute-done.9.refs_1_, ...), custom_call_target="tpu_custom_call" | custom-call | flops 7000000000 | bytes 1024 | tf_op jit(solution)/shard_map/chebyshev/pallas_call | solution.py:71
  88.4 0.1 collective-permute-start.13
  88.5 0.3 collective-permute-start.14
  88.9 0.0 collective-permute-done.16.refs_1_
  88.9 1.8 %collective-permute-start.15 = (bf16[64,512]{1,0:T(8,128)(2,1)S(1)}, bf16[64,512]{1,0:T(8,128)(2,1)S(1)}, u32[]{:S(2)}, u32[]{:S(2)}) collective-permute-start(bf16[64,512]{1,0:T(8,128)(2,1)S(1)} %get-tuple-element.67), channel_id=1, source_target_pairs={{0,3},{1,2},{2,1},{3,0},{4,7},{5,6},{6,5},{7,4},{8,11},{9,10},{10,... | collective-permute-start | bytes 196616 | tf_op jit(solution)/shard_map/ppermute | solution.py:255
  90.7 0.0 collective-permute-done.17.refs_2_
  90.7 0.0 collective-permute-done.18.refs_3_
  90.7 4.0 %clean.2 = (f32[256,1024]{1,0:T(8,128)}, f32[8,1024]{1,0:T(8,128)S(1)}, f32[8,128]{1,0:T(8,128)S(1)}) custom-call(f32[32,512]{1,0:T(8,128)S(1)} %get-tuple-element.70.refs_0_, bf16[32,512]{1,0:T(8,128)(2,1)S(1)} %collective-permute-done.16.refs_1_, bf16[32,512]{1,0:T(8,128)(2,1)S(1)} %collective-permute-done.17.refs_2_, ...), custom_call_target="tpu_custom_call" | custom-call | flops 1500000000 | bytes 1024 | tf_op jit(solution)/shard_map/clean/pallas_call | solution.py:71
  94.7 0.0 collective-permute-done.13.refs_1_
  94.7 0.0 collective-permute-done.14.refs_2_
  94.7 0.0 collective-permute-done.15.refs_3_
  94.7 3.0 %clean.3 = (f32[8,1024]{1,0:T(8,128)}, f32[8,128]{1,0:T(8,128)}) custom-call(f32[64,512]{1,0:T(8,128)S(1)} %get-tuple-element.66.refs_0_, bf16[64,512]{1,0:T(8,128)(2,1)S(1)} %collective-permute-done.13.refs_1_, bf16[64,512]{1,0:T(8,128)(2,1)S(1)} %collective-permute-done.14.refs_2_, bf16[64,512]{1,0:T(8,128)(2,1)S(1)} %collective-permute-done.15.refs_3_, ...), custom_call_target="tpu_custom_call" | custom-call | flops 1500000000 | bytes 1024 | tf_op jit(solution)/shard_map/clean/pallas_call | solution.py:71
Async XLA Ops:
  0.6 16.8 %collective-permute-start = (bf16[32,8,1024]{2,1,0:T(8,128)(2,1)}, bf16[32,8,1024]{2,1,0:T(8,128)(2,1)S(1)}, u32[]{:S(2)}, u32[]{:S(2)}) collective-permute-start(bf16[32,8,1024]{2,1,0:T(8,128)(2,1)} %param.4), channel_id=1, source_target_pairs={{0,8},{4,12},{8,16},{12,20},{16,24},{20,28},{24,32},{28,36},{32,40... | collective-permute-start | bytes 1572872 | tf_op jit(solution)/shard_map/ppermute | solution.py:465
  2.3 41.3 %collective-permute-start.1 = (bf16[32,8,1024]{2,1,0:T(8,128)(2,1)}, bf16[32,8,1024]{2,1,0:T(8,128)(2,1)S(1)}, u32[]{:S(2)}, u32[]{:S(2)}) collective-permute-start(bf16[32,8,1024]{2,1,0:T(8,128)(2,1)} %param.4), channel_id=1, source_target_pairs={{0,4},{8,12},{16,20},{24,28},{32,36},{40,44},{48,52},{56,60},{64,6... | collective-permute-start | bytes 1572872 | tf_op jit(solution)/shard_map/ppermute | solution.py:465
  3.6 8.7 %copy-start.1 = (f32[1,8,1024]{2,1,0:T(8,128)S(1)}, f32[1,8,1024]{2,1,0:T(8,128)}, u32[]{:S(2)}) copy-start(f32[1,8,1024]{2,1,0:T(8,128)} %param.7) | copy-start | bytes 98308
  3.6 8.7 %copy-start.2 = (s32[1,1024]{1,0:T(1,128)S(1)}, s32[1,1024]{1,0:T(1,128)}, u32[]{:S(2)}) copy-start(s32[1,1024]{1,0:T(1,128)} %refs_0_.1) | copy-start | bytes 12292
  12.3 1.9 %copy-start = (bf16[32,8,1024]{2,1,0:T(8,128)(2,1)S(1)}, bf16[32,8,1024]{2,1,0:T(8,128)(2,1)}, u32[]{:S(2)}) copy-start(bf16[32,8,1024]{2,1,0:T(8,128)(2,1)} %param.4) | copy-start | bytes 1572868
  17.4 26.2 %collective-permute-start.2 = (bf16[32,8,1024]{2,1,0:T(8,128)(2,1)S(1)}, bf16[32,8,1024]{2,1,0:T(8,128)(2,1)S(1)}, u32[]{:S(2)}, u32[]{:S(2)}) collective-permute-start(bf16[32,8,1024]{2,1,0:T(8,128)(2,1)S(1)} %collective-permute-done), channel_id=1, source_target_pairs={{4,0},{12,8},{20,16},{28,24},{36,32},{44,40},{52,48},{60,56},{68,6... | collective-permute-start | bytes 1572872 | tf_op jit(solution)/shard_map/ppermute | solution.py:465
  23.0 3.3 %collective-permute-start.3 = (bf16[32,512]{1,0:T(8,128)(2,1)S(1)}, bf16[32,512]{1,0:T(8,128)(2,1)S(1)}, u32[]{:S(2)}, u32[]{:S(2)}) collective-permute-start(bf16[32,512]{1,0:T(8,128)(2,1)S(1)} %get-tuple-element.47), channel_id=1, source_target_pairs={{0,1},{1,0},{2,3},{3,2},{4,5},{5,4},{6,7},{7,6},{8,9},{9,8},{10,11... | collective-permute-start | bytes 98312 | tf_op jit(solution)/shard_map/ppermute | solution.py:255
  24.6 10.6 %collective-permute-start.4 = (bf16[32,512]{1,0:T(8,128)(2,1)S(1)}, bf16[32,512]{1,0:T(8,128)(2,1)S(1)}, u32[]{:S(2)}, u32[]{:S(2)}) collective-permute-start(bf16[32,512]{1,0:T(8,128)(2,1)S(1)} %get-tuple-element.47), channel_id=1, source_target_pairs={{0,2},{1,3},{2,0},{3,1},{4,6},{5,7},{6,4},{7,5},{8,10},{9,11},{10,... | collective-permute-start | bytes 98312 | tf_op jit(solution)/shard_map/ppermute | solution.py:255
  25.6 11.9 %collective-permute-start.5 = (bf16[32,512]{1,0:T(8,128)(2,1)S(1)}, bf16[32,512]{1,0:T(8,128)(2,1)S(1)}, u32[]{:S(2)}, u32[]{:S(2)}) collective-permute-start(bf16[32,512]{1,0:T(8,128)(2,1)S(1)} %get-tuple-element.47), channel_id=1, source_target_pairs={{0,3},{1,2},{2,1},{3,0},{4,7},{5,6},{6,5},{7,4},{8,11},{9,10},{10,... | collective-permute-start | bytes 98312 | tf_op jit(solution)/shard_map/ppermute | solution.py:255
  39.1 23.8 %collective-permute-start.11 = (bf16[6,48,1024]{2,1,0:T(8,128)(2,1)S(1)}, bf16[6,48,1024]{2,1,0:T(8,128)(2,1)S(1)}, u32[]{:S(2)}, u32[]{:S(2)}) collective-permute-start(bf16[6,48,1024]{2,1,0:T(8,128)(2,1)S(1)} %get-tuple-element.60), channel_id=1, source_target_pairs={{0,1},{1,2},{2,3},{4,5},{5,6},{6,7},{8,9},{9,10},{10,11},{12,13},{... | collective-permute-start | bytes 1769480 | tf_op jit(solution)/shard_map/ppermute | solution.py:493
  41.7 21.2 %collective-permute-start.12 = (bf16[6,48,1024]{2,1,0:T(8,128)(2,1)S(1)}, bf16[6,48,1024]{2,1,0:T(8,128)(2,1)S(1)}, u32[]{:S(2)}, u32[]{:S(2)}) collective-permute-start(bf16[6,48,1024]{2,1,0:T(8,128)(2,1)S(1)} %get-tuple-element.61), channel_id=1, source_target_pairs={{1,0},{2,1},{3,2},{5,4},{6,5},{7,6},{9,8},{10,9},{11,10},{13,12},{... | collective-permute-start | bytes 1769480 | tf_op jit(solution)/shard_map/ppermute | solution.py:494
  47.7 2.2 %collective-permute-start.6 = (bf16[64,512]{1,0:T(8,128)(2,1)S(1)}, bf16[64,512]{1,0:T(8,128)(2,1)S(1)}, u32[]{:S(2)}, u32[]{:S(2)}) collective-permute-start(bf16[64,512]{1,0:T(8,128)(2,1)S(1)} %get-tuple-element.53), channel_id=1, source_target_pairs={{0,1},{1,0},{2,3},{3,2},{4,5},{5,4},{6,7},{7,6},{8,9},{9,8},{10,11... | collective-permute-start | bytes 196616 | tf_op jit(solution)/shard_map/ppermute | solution.py:255
  47.8 4.2 %collective-permute-start.7 = (bf16[64,512]{1,0:T(8,128)(2,1)S(1)}, bf16[64,512]{1,0:T(8,128)(2,1)S(1)}, u32[]{:S(2)}, u32[]{:S(2)}) collective-permute-start(bf16[64,512]{1,0:T(8,128)(2,1)S(1)} %get-tuple-element.53), channel_id=1, source_target_pairs={{0,2},{1,3},{2,0},{3,1},{4,6},{5,7},{6,4},{7,5},{8,10},{9,11},{10,... | collective-permute-start | bytes 196616 | tf_op jit(solution)/shard_map/ppermute | solution.py:255
  49.6 6.1 %collective-permute-start.8 = (bf16[64,512]{1,0:T(8,128)(2,1)S(1)}, bf16[64,512]{1,0:T(8,128)(2,1)S(1)}, u32[]{:S(2)}, u32[]{:S(2)}) collective-permute-start(bf16[64,512]{1,0:T(8,128)(2,1)S(1)} %get-tuple-element.53), channel_id=1, source_target_pairs={{0,3},{1,2},{2,1},{3,0},{4,7},{5,6},{6,5},{7,4},{8,11},{9,10},{10,... | collective-permute-start | bytes 196616 | tf_op jit(solution)/shard_map/ppermute | solution.py:255
  57.3 16.7 %collective-permute-start.10 = (bf16[6,64,1024]{2,1,0:T(8,128)(2,1)S(1)}, bf16[6,64,1024]{2,1,0:T(8,128)(2,1)S(1)}, u32[]{:S(2)}, u32[]{:S(2)}) collective-permute-start(bf16[6,64,1024]{2,1,0:T(8,128)(2,1)S(1)} %get-tuple-element.58), channel_id=1, source_target_pairs={{1,0},{2,1},{3,2},{5,4},{6,5},{7,6},{9,8},{10,9},{11,10},{13,12},{... | collective-permute-start | bytes 2359304 | tf_op jit(solution)/shard_map/ppermute | solution.py:494
  59.3 14.8 %collective-permute-start.9 = (bf16[6,64,1024]{2,1,0:T(8,128)(2,1)S(1)}, bf16[6,64,1024]{2,1,0:T(8,128)(2,1)S(1)}, u32[]{:S(2)}, u32[]{:S(2)}) collective-permute-start(bf16[6,64,1024]{2,1,0:T(8,128)(2,1)S(1)} %get-tuple-element.57), channel_id=1, source_target_pairs={{0,1},{1,2},{2,3},{4,5},{5,6},{6,7},{8,9},{9,10},{10,11},{12,13},{... | collective-permute-start | bytes 2359304 | tf_op jit(solution)/shard_map/ppermute | solution.py:493
  71.9 17.0 %collective-permute-start.16 = (bf16[32,512]{1,0:T(8,128)(2,1)S(1)}, bf16[32,512]{1,0:T(8,128)(2,1)S(1)}, u32[]{:S(2)}, u32[]{:S(2)}) collective-permute-start(bf16[32,512]{1,0:T(8,128)(2,1)S(1)} %get-tuple-element.71), channel_id=1, source_target_pairs={{0,1},{1,0},{2,3},{3,2},{4,5},{5,4},{6,7},{7,6},{8,9},{9,8},{10,11... | collective-permute-start | bytes 98312 | tf_op jit(solution)/shard_map/ppermute | solution.py:255
  71.9 18.7 %collective-permute-start.17 = (bf16[32,512]{1,0:T(8,128)(2,1)S(1)}, bf16[32,512]{1,0:T(8,128)(2,1)S(1)}, u32[]{:S(2)}, u32[]{:S(2)}) collective-permute-start(bf16[32,512]{1,0:T(8,128)(2,1)S(1)} %get-tuple-element.71), channel_id=1, source_target_pairs={{0,2},{1,3},{2,0},{3,1},{4,6},{5,7},{6,4},{7,5},{8,10},{9,11},{10,... | collective-permute-start | bytes 98312 | tf_op jit(solution)/shard_map/ppermute | solution.py:255
  72.0 18.6 %collective-permute-start.18 = (bf16[32,512]{1,0:T(8,128)(2,1)S(1)}, bf16[32,512]{1,0:T(8,128)(2,1)S(1)}, u32[]{:S(2)}, u32[]{:S(2)}) collective-permute-start(bf16[32,512]{1,0:T(8,128)(2,1)S(1)} %get-tuple-element.71), channel_id=1, source_target_pairs={{0,3},{1,2},{2,1},{3,0},{4,7},{5,6},{6,5},{7,4},{8,11},{9,10},{10,... | collective-permute-start | bytes 98312 | tf_op jit(solution)/shard_map/ppermute | solution.py:255
  88.4 6.2 %collective-permute-start.13 = (bf16[64,512]{1,0:T(8,128)(2,1)S(1)}, bf16[64,512]{1,0:T(8,128)(2,1)S(1)}, u32[]{:S(2)}, u32[]{:S(2)}) collective-permute-start(bf16[64,512]{1,0:T(8,128)(2,1)S(1)} %get-tuple-element.67), channel_id=1, source_target_pairs={{0,1},{1,0},{2,3},{3,2},{4,5},{5,4},{6,7},{7,6},{8,9},{9,8},{10,11... | collective-permute-start | bytes 196616 | tf_op jit(solution)/shard_map/ppermute | solution.py:255
  88.5 6.2 %collective-permute-start.14 = (bf16[64,512]{1,0:T(8,128)(2,1)S(1)}, bf16[64,512]{1,0:T(8,128)(2,1)S(1)}, u32[]{:S(2)}, u32[]{:S(2)}) collective-permute-start(bf16[64,512]{1,0:T(8,128)(2,1)S(1)} %get-tuple-element.67), channel_id=1, source_target_pairs={{0,2},{1,3},{2,0},{3,1},{4,6},{5,7},{6,4},{7,5},{8,10},{9,11},{10,... | collective-permute-start | bytes 196616 | tf_op jit(solution)/shard_map/ppermute | solution.py:255
  88.9 5.8 %collective-permute-start.15 = (bf16[64,512]{1,0:T(8,128)(2,1)S(1)}, bf16[64,512]{1,0:T(8,128)(2,1)S(1)}, u32[]{:S(2)}, u32[]{:S(2)}) collective-permute-start(bf16[64,512]{1,0:T(8,128)(2,1)S(1)} %get-tuple-element.67), channel_id=1, source_target_pairs={{0,3},{1,2},{2,1},{3,0},{4,7},{5,6},{6,5},{7,4},{8,11},{9,10},{10,... | collective-permute-start | bytes 196616 | tf_op jit(solution)/shard_map/ppermute | solution.py:255

commit v2 on v1

--- a/solution.py
+++ b/solution.py
@@ -230,7 +230,8 @@
     for b, count in enumerate(counts):
         value = sources[0][...]
         if count == 2:
-            value = value + sources[1][...]
+            odd = lax.axis_index("group") % 2 == 1
+            value = jnp.where(odd, value, sources[1][...])
         sources = sources[count:]
         got = dot(dot(perm, value).astype(BF16), pick_ref[...]).astype(BF16)
         out_ref[:, b * BATCH : (b + 1) * BATCH, :] = got.reshape(SLAB, BATCH, PLANE)
@@ -301,15 +302,15 @@
 DOWN = [(j, i) for i, j in UP]
 
 
-def filter_kernel(given, *refs):
-    field_ref, below_ref, above_ref, core_ref = refs[:4]
-    if given:
-        weight_ref, flag_ref, out_ref, full_ref, half_ref = refs[4:9]
+def filter_kernel(ahead, *refs):
+    field_ref, below_ref, above_ref = refs[:3]
+    if ahead:
+        local_ref, weight_ref, first_ref, flag_ref, out_ref = refs[3:8]
     else:
-        local_ref, weight_ref, flag_ref, out_ref, full_ref, half_ref = refs[4:10]
+        weight_ref, first_ref, flag_ref, core_ref, other_ref, out_ref, full_ref, half_ref = refs[3:11]
     below, above, even, odd = refs[-4:]
     rows = field_ref.shape[1]
-    if not given:
+    if ahead:
         weight_ref[HALO : HALO + SLAB] = 8.0 * local_ref[...] - 2.0
         for k, ref in enumerate((below_ref, above_ref)):
             for x in range(HALO):
@@ -319,6 +320,7 @@
                 weight_ref[place : place + 1] = 8.0 * near - 2.0
                 if x == 0:
                     flag_ref[k] = jnp.broadcast_to(extra[3:4, :LANES], (8, LANES))
+        first_ref[...] = weight_ref[...] - EK[KDEG - 1]
     lane = iota((8, LANES), 1)
     head, tail = lane < 16, lane >= LANES - 16
     first_z, last_z = lane % 16 == 0, lane % 16 == 15
@@ -359,8 +361,11 @@
                     mate = here[j ^ 1]
                     z = mate + (rolled(first_z, mate, -1) if j % 2 else rolled(last_z, mate, 1))
                     around = (before[j] + after[j]) + (above_y + below_y) + z
-                    w = jnp.broadcast_to(weight_ref[pl.ds(x, 1), lanes], (8, LANES))
-                    value = around - w * c + EK[KDEG - k] * begin(x, lanes)
+                    w_ref = first_ref if k == 1 else weight_ref
+                    w = jnp.broadcast_to(w_ref[pl.ds(x, 1), lanes], (8, LANES))
+                    value = around - w * c
+                    if k > 1:
+                        value = value + EK[KDEG - k] * begin(x, lanes)
                     if x == HALO - 1:
                         value = value * low_flag
                     elif x == HALO + SLAB:
@@ -384,28 +389,44 @@
                 pl.ds(pl.multiple_of(i * 16 + k * 8, 8), 8),
             )
 
-    sums(lambda x: out_ref[x].astype(BF16), core_ref, full_ref, half_ref)
-
-
-def chebyshev(line, field, below, above, core_x, local, weight):
+    if not ahead:
+
+        def both_of(x):
+            return jnp.concatenate([other_ref[x].astype(BF16), out_ref[x].astype(BF16)], axis=0)
+
+        sums(both_of, core_ref, full_ref, half_ref)
+
+
+def filter_scratch():
+    halo, whole = pltpu.VMEM((HALO, 16, PLANE), F32), pltpu.VMEM((WIDE, 8, PLANE), F32)
+    return [halo, halo, whole, whole]
+
+
+def filter_ahead(line, field, below, above, local):
     rows = field.shape[1]
-    made = (struct((WIDE, PLANE), F32), struct((2, 8, LANES), F32))
-    given = weight is not None
+    wide = struct((WIDE, PLANE), F32)
     got = line.call(
-        lambda *refs: filter_kernel(given, *refs),
-        "chebyshev",
-        (() if given else made)
-        + (struct((SLAB, rows, PLANE), F32), struct((rows, NCORE), F32), struct((rows, NCORE), BF16)),
-        (field, below, above, core_x) + (tuple(weight) if given else (local,)),
-        scratch=[
-            pltpu.VMEM((HALO, 16, PLANE), F32),
-            pltpu.VMEM((HALO, 16, PLANE), F32),
-            pltpu.VMEM((WIDE, 8, PLANE), F32),
-            pltpu.VMEM((WIDE, 8, PLANE), F32),
-        ],
-        micros=2 + rows // 5,
-    )
-    return (weight, got) if given else (got[:2], got[2:])
+        lambda *refs: filter_kernel(True, *refs),
+        "filter_ahead",
+        (wide, wide, struct((2, 8, LANES), F32), struct((SLAB, rows, PLANE), F32)),
+        (field, below, above, local),
+        scratch=filter_scratch(),
+        micros=7,
+    )
+    return got[:3], got[3]
+
+
+def filter_rest(line, field, below, above, weight, core_x, ahead):
+    rows = field.shape[1]
+    total = rows + ahead.shape[1]
+    return line.call(
+        lambda *refs: filter_kernel(False, *refs),
+        "filter_rest",
+        (struct((SLAB, rows, PLANE), F32), struct((total, NCORE), F32), struct((total, NCORE), BF16)),
+        (field, below, above, *weight, core_x, ahead),
+        scratch=filter_scratch(),
+        micros=14,
+    )
 
 
 def reorder(value, order_ref):
@@ -413,52 +434,36 @@
     return dot(parts[0], order_ref[...]) + dot(parts[1], order_ref[...])
 
 
-def clean_kernel(first, last, *refs):
-    refs = list(refs)
-    full_ref, a_ref, b_ref, c_ref, field_ref, mapped_ref, core_ref = refs[:7]
-    refs = refs[7:]
-    order_ref = refs.pop(0) if first or last else None
-    before_ref = None if first else refs.pop(0)
-    own_ref = refs.pop(0) if first else None
-    density_ref = refs.pop(0)
-    own = refs.pop(0) if first else None
-    rows = refs.pop(0)
+def clean_kernel(full_ref, a_ref, b_ref, c_ref, ahead_ref, rest_ref, mapped_ref, mapped_rest_ref, core_ref, order_ref, own_ref, density_ref, own, rows):
     coef = total_of(full_ref, a_ref, b_ref, c_ref)
     for x in range(SLAB):
-        value = field_ref[x] - dot(coef, core_ref[x])
-        if first:
-            own[x * BATCH : (x + 1) * BATCH] = value[:BATCH]
-        weighted = jnp.sum(mapped_ref[x].astype(F32) * value, axis=0, keepdims=True)
+        taken = dot(coef, core_ref[x])
+        ahead = ahead_ref[x] - taken[:BATCH]
+        rest = rest_ref[x] - taken[BATCH:]
+        own[x * BATCH : (x + 1) * BATCH] = ahead
+        weighted = jnp.sum(mapped_ref[x].astype(F32) * ahead, axis=0, keepdims=True)
+        weighted += jnp.sum(mapped_rest_ref[x].astype(F32) * rest, axis=0, keepdims=True)
         rows[x : x + 1] = weighted / (3.0 * BATCH)
-    if first:
-        back = row_permutation(BATCH * SLAB, BATCH)
-        total = None
-        for part in split(own[...], 2):
-            moved = dot(dot(back, part).astype(BF16), order_ref[...])
-            total = moved if total is None else total + moved
-        own_ref[...] = total
-    density = rows[...] if first else rows[...] + before_ref[...]
-    density_ref[...] = reorder(density, order_ref) if last else density
-
-
-def clean(line, full, others, field, mapped, core_x, order, density, first, last):
-    args = [full, *others, field, mapped, core_x]
-    if first or last:
-        args.append(order)
-    if not first:
-        args.append(density)
-    small = struct((SLAB, PLANE), F32)
-    own = struct((SLAB * BATCH, PLANE), F32)
-    got = line.call(
-        lambda *refs: clean_kernel(first, last, *refs),
+    back = row_permutation(BATCH * SLAB, BATCH)
+    total = None
+    for part in split(own[...], 2):
+        moved = dot(dot(back, part).astype(BF16), order_ref[...])
+        total = moved if total is None else total + moved
+    own_ref[...] = total
+    density_ref[...] = reorder(rows[...], order_ref)
+
+
+def clean(line, full, others, ahead, rest, mapped, mapped_rest, core_x, order):
+    small, own = struct((SLAB, PLANE), F32), struct((SLAB * BATCH, PLANE), F32)
+    return line.call(
+        clean_kernel,
         "clean",
-        (own, small) if first else (small,),
-        args,
-        scratch=([pltpu.VMEM(own.shape, F32)] if first else []) + [pltpu.VMEM(small.shape, F32)],
+        (own, small),
+        (full, *others, ahead, rest, mapped, mapped_rest, core_x, order),
+        scratch=[pltpu.VMEM(own.shape, F32), pltpu.VMEM(small.shape, F32)],
         limit=12,
-        micros=3,
-    )
-    return (got[0], got[1]) if first else (None, got[0])
+        micros=4,
+    )
 
 
 def permute_groups(array, pairs):
@@ -467,57 +472,30 @@
 
 def body(stochastic, plane_map, core_orbitals, potential):
     groups = lax.axis_size("group")
+    mate = permute_groups(stochastic, [(i, i ^ 1) for i in range(groups)])
     third = permute_groups(stochastic, [(i, (i + 2) % groups) for i in range(groups)])
-    to_odd = permute_groups(stochastic, [(i, i + 1) for i in range(0, groups, 2)])
-    to_even = None
 
     line = Line()
     core_x = relayout(line, core_orbitals[0])
     order, pick, local = prepare(line, plane_map, potential[0])
-    state = {}
-    weight = density = own = None
-    for step, c in PLAN:
-        s = state.setdefault(c, {})
-        if step == "forward":
-            third, line.token = lax.optimization_barrier((third, line.token))
-            to_even = permute_groups(third, [(i + 1, i) for i in range(0, groups, 2)])
-        elif step == "map":
-            batches = [(stochastic,), (to_odd, to_even), (third,)]
-            visits = [batches[t] for t in VISITS[c]]
-            s["mapped"], s["full"], half = map_batches(line, pick, core_x, visits)
-            s["others"] = exchange(half)
-        elif step == "project":
-            s["field"], low, high = project(
-                line, s["full"], s["others"], s["mapped"], core_x, local if c == 0 else None
-            )
-            s["below"] = lax.ppermute(high, "grid", UP)
-            s["above"] = lax.ppermute(low, "grid", DOWN)
-        elif step == "filter":
-            weight, (s["done"], s["full"], half) = chebyshev(
-                line, s["field"], s["below"], s["above"], core_x, local, weight
-            )
-            s["others"] = exchange(half)
-        elif step == "clean":
-            got, density = clean(
-                line, s["full"], s["others"], s["done"], s["mapped"], core_x, order, density,
-                c == 0, c == len(VISITS) - 1,
-            )
-            own = got if c == 0 else own
+
+    mapped, full, half = map_batches(line, pick, core_x, [(stochastic,)])
+    others = exchange(half)
+    mate, line.token = lax.optimization_barrier((mate, line.token))
+    second = permute_groups(mate, [(i, (i + 2) % groups) for i in range(0, groups, 2)])
+    field, low, high = project(line, full, others, mapped, core_x, local)
+    below, above = lax.ppermute(high, "grid", UP), lax.ppermute(low, "grid", DOWN)
+
+    mapped_rest, full, half = map_batches(line, pick, core_x, [(third,), (mate, second)])
+    rest, low, high = project(line, full, exchange(half), mapped_rest, core_x, None)
+    below_rest, above_rest = lax.ppermute(high, "grid", UP), lax.ppermute(low, "grid", DOWN)
+
+    weight, ahead = filter_ahead(line, field, below, above, local)
+    rest, full, half = filter_rest(line, rest, below_rest, above_rest, weight, core_x, ahead)
+    own, density = clean(
+        line, full, exchange(half), ahead, rest, mapped, mapped_rest, core_x, order
+    )
     return density[None], own.reshape(BATCH, SLAB, PLANE)
-
-
-VISITS = ((0,), (2, 1))
-PLAN = (
-    ("map", 0),
-    ("forward", 0),
-    ("project", 0),
-    ("map", 1),
-    ("project", 1),
-    ("filter", 0),
-    ("filter", 1),
-    ("clean", 0),
-    ("clean", 1),
-)
 
 
 def solution(mesh):

time: 97.9 us -> 91.2 us (0.932)
  the two profiles are of different devices: /device:TPU:23 before, /device:TPU:0 now
where the time goes in v2:
time: 91.2 us; the launch traced here: 91 us
  Pallas kernels  43.8 us (48%)
  starting transfers between devices  31.2 us (34%)
  waiting for transfers between devices  15.2 us (17%)
    pallas_call x9, Pallas kernels, call(): pl.pallas_call(with_token, in_specs=specs, out_specs=tuple((VMEM for _ in...  43.8 us
    ppermute x9, starting transfers between devices, exchange(): lax.ppermute(half, 'grid', [(i, i ^ k) for i in range(GRID)])  14 us
    ppermute x3, starting transfers between devices, permute_groups(): return lax.ppermute(array, 'group', pairs)  9.11 us
    ppermute x3, waiting for transfers between devices, permute_groups(): return lax.ppermute(array, 'group', pairs)  8.75 us
    ppermute x9, waiting for transfers between devices, exchange(): lax.ppermute(half, 'grid', [(i, i ^ k) for i in range(GRID)])  6.45 us
    ppermute x2, starting transfers between devices, body(): lax.ppermute(high, 'grid', UP)  5.27 us
    ppermute x2, starting transfers between devices, body(): lax.ppermute(low, 'grid', DOWN)  2.76 us
  transfers between devices with their start and end apart: 16, of which 4 were waited for; matrix products, arithmetic and copies ran while one was open for 0% of the time, Pallas kernels for 24%

profile of v2, /device:TPU:0, one launch (start us, length us, event | category | flops | bytes accessed | tf_op | source)
XLA Modules:
  0.0 91.0 jit_solution(12345809404771968597)
XLA Ops:
  0.6 2.1 %collective-permute-start = (bf16[32,8,1024]{2,1,0:T(8,128)(2,1)}, bf16[32,8,1024]{2,1,0:T(8,128)(2,1)S(1)}, u32[]{:S(2)}, u32[]{:S(2)}) collective-permute-start(bf16[32,8,1024]{2,1,0:T(8,128)(2,1)} %param.4), channel_id=1, source_target_pairs={{0,8},{4,12},{8,16},{12,20},{16,24},{20,28},{24,32},{28,36},{32,40... | collective-permute-start | bytes 1572872 | tf_op jit(solution)/shard_map/ppermute | solution.py:470
  2.7 3.2 %collective-permute-start.1 = (bf16[32,8,1024]{2,1,0:T(8,128)(2,1)}, bf16[32,8,1024]{2,1,0:T(8,128)(2,1)S(1)}, u32[]{:S(2)}, u32[]{:S(2)}) collective-permute-start(bf16[32,8,1024]{2,1,0:T(8,128)(2,1)} %param.4), channel_id=1, source_target_pairs={{0,4},{4,0},{8,12},{12,8},{16,20},{20,16},{24,28},{28,24},{32,36},... | collective-permute-start | bytes 1572872 | tf_op jit(solution)/shard_map/ppermute | solution.py:470
  5.9 0.0 copy-start.1
  5.9 0.0 copy-start.2
  5.9 8.6 %relayout.1 = (bf16[8,512,1024]{2,1,0:T(8,128)(2,1)S(1)}, f32[8,128]{1,0:T(8,128)S(1)}) custom-call(bf16[4096,1024]{1,0:T(8,128)(2,1)} %bitcast.13), custom_call_target="tpu_custom_call" | custom-call | flops 4000000000 | bytes 1024 | tf_op jit(solution)/shard_map/relayout/pallas_call | solution.py:71
  14.6 0.0 copy-start
  14.6 0.0 copy-done.1
  14.6 0.0 copy-done.2
  14.6 1.8 %prepare.1 = (bf16[1024,1024]{1,0:T(8,128)(2,1)S(1)}, bf16[1024,1024]{1,0:T(8,128)(2,1)S(1)}, f32[8,1024]{1,0:T(8,128)S(1)}, f32[8,128]{1,0:T(8,128)S(1)}) custom-call(s32[1,1024]{1,0:T(1,128)S(1)} %copy-done.2, f32[8,1024]{1,0:T(8,128)S(1)} %bitcast.12, f32[8,128]{1,0:T(8,128)S(1)} %get-tuple-element.37.refs_2_), custom_call_target="tpu_custom_call" | custom-call | flops 1000000000 | bytes 1024 | tf_op jit(solution)/shard_map/prepare/pallas_call | solution.py:71
  16.4 0.0 copy-done
  16.4 3.2 %map_batches.2 = (bf16[8,32,1024]{2,1,0:T(8,128)(2,1)S(1)}, f32[32,512]{1,0:T(8,128)S(1)}, bf16[32,512]{1,0:T(8,128)(2,1)S(1)}, f32[8,128]{1,0:T(8,128)S(1)}) custom-call(bf16[1024,1024]{1,0:T(8,128)(2,1)S(1)} %get-tuple-element.38.refs_0_, bf16[8,512,1024]{2,1,0:T(8,128)(2,1)S(1)} %get-tuple-element.39.refs_1_.refs_5_.refs_6_.refs_8_, ...), custom_call_target="tpu_custom_call" | custom-call | flops 1000000000 | bytes 1024 | tf_op jit(solution)/shard_map/map_batches/pallas_call | solution.py:71
  19.7 0.0 collective-permute-done.1
  19.7 3.8 %collective-permute-start.2 = (bf16[32,8,1024]{2,1,0:T(8,128)(2,1)S(1)}, bf16[32,8,1024]{2,1,0:T(8,128)(2,1)S(1)}, u32[]{:S(2)}, u32[]{:S(2)}) collective-permute-start(bf16[32,8,1024]{2,1,0:T(8,128)(2,1)S(1)} %collective-permute-done.1), channel_id=1, source_target_pairs={{0,8},{8,16},{16,24},{24,32},{32,40},{40,48},{48,56},{56,64},{64,7... | collective-permute-start | bytes 1572872 | tf_op jit(solution)/shard_map/ppermute | solution.py:470
  23.5 0.1 collective-permute-start.5
  23.6 0.8 collective-permute-start.4
  24.4 1.1 %collective-permute-start.3 = (bf16[32,512]{1,0:T(8,128)(2,1)S(1)}, bf16[32,512]{1,0:T(8,128)(2,1)S(1)}, u32[]{:S(2)}, u32[]{:S(2)}) collective-permute-start(bf16[32,512]{1,0:T(8,128)(2,1)S(1)} %get-tuple-element.44), channel_id=1, source_target_pairs={{0,1},{1,0},{2,3},{3,2},{4,5},{5,4},{6,7},{7,6},{8,9},{9,8},{10,11... | collective-permute-start | bytes 98312 | tf_op jit(solution)/shard_map/ppermute | solution.py:256
  25.5 1.5 %collective-permute-done.5.refs_3_ = bf16[32,512]{1,0:T(8,128)(2,1)S(1)} collective-permute-done((bf16[32,512]{1,0:T(8,128)(2,1)S(1)}, bf16[32,512]{1,0:T(8,128)(2,1)S(1)}, u32[]{:S(2)}, u32[]{:S(2)}) %collective-permute-start.5) | collective-permute-done | bytes 32800 | tf_op jit(solution)/shard_map/ppermute | solution.py:256
  27.0 0.7 collective-permute-done.4.refs_2_
  27.7 0.0 collective-permute-done.3.refs_1_
  27.7 1.6 %project.2 = (f32[8,32,1024]{2,1,0:T(8,128)S(1)}, bf16[6,48,1024]{2,1,0:T(8,128)(2,1)S(1)}, bf16[6,48,1024]{2,1,0:T(8,128)(2,1)S(1)}, f32[8,128]{1,0:T(8,128)S(1)}) custom-call(f32[32,512]{1,0:T(8,128)S(1)} %get-tuple-element.43.refs_0_, bf16[32,512]{1,0:T(8,128)(2,1)S(1)} %collective-permute-done.3.refs_1_, ...), custom_call_target="tpu_custom_call" | custom-call | flops 1000000000 | bytes 1024 | tf_op jit(solution)/shard_map/project/pallas_call | solution.py:71
  29.3 0.0 collective-permute-done
  29.3 8.7 %collective-permute-done.2 = bf16[32,8,1024]{2,1,0:T(8,128)(2,1)S(1)} collective-permute-done((bf16[32,8,1024]{2,1,0:T(8,128)(2,1)S(1)}, bf16[32,8,1024]{2,1,0:T(8,128)(2,1)S(1)}, u32[]{:S(2)}, u32[]{:S(2)}) %collective-permute-start.2) | collective-permute-done | bytes 524320 | tf_op jit(solution)/shard_map/ppermute | solution.py:470
  38.0 4.1 %map_batches.3 = (bf16[8,64,1024]{2,1,0:T(8,128)(2,1)S(1)}, f32[64,512]{1,0:T(8,128)S(1)}, bf16[64,512]{1,0:T(8,128)(2,1)S(1)}, f32[8,128]{1,0:T(8,128)S(1)}) custom-call(bf16[1024,1024]{1,0:T(8,128)(2,1)S(1)} %get-tuple-element.38.refs_0_, bf16[8,512,1024]{2,1,0:T(8,128)(2,1)S(1)} %get-tuple-element.39.refs_1_.refs_5_.refs_6_.refs_8_, ...), custom_call_target="tpu_custom_call" | custom-call | flops 1500000000 | bytes 1024 | tf_op jit(solution)/shard_map/map_batches/pallas_call | solution.py:71
  42.1 0.1 collective-permute-start.8
  42.2 0.8 collective-permute-start.7
  42.9 1.1 %collective-permute-start.6 = (bf16[64,512]{1,0:T(8,128)(2,1)S(1)}, bf16[64,512]{1,0:T(8,128)(2,1)S(1)}, u32[]{:S(2)}, u32[]{:S(2)}) collective-permute-start(bf16[64,512]{1,0:T(8,128)(2,1)S(1)} %get-tuple-element.50), channel_id=1, source_target_pairs={{0,1},{1,0},{2,3},{3,2},{4,5},{5,4},{6,7},{7,6},{8,9},{9,8},{10,11... | collective-permute-start | bytes 196616 | tf_op jit(solution)/shard_map/ppermute | solution.py:256
  44.0 1.9 %collective-permute-start.11 = (bf16[6,48,1024]{2,1,0:T(8,128)(2,1)S(1)}, bf16[6,48,1024]{2,1,0:T(8,128)(2,1)S(1)}, u32[]{:S(2)}, u32[]{:S(2)}) collective-permute-start(bf16[6,48,1024]{2,1,0:T(8,128)(2,1)S(1)} %get-tuple-element.57), channel_id=1, source_target_pairs={{0,1},{1,2},{2,3},{4,5},{5,6},{6,7},{8,9},{9,10},{10,11},{12,13},{... | collective-permute-start | bytes 1769480 | tf_op jit(solution)/shard_map/ppermute | solution.py:487
  46.0 1.5 %collective-permute-start.12 = (bf16[6,48,1024]{2,1,0:T(8,128)(2,1)S(1)}, bf16[6,48,1024]{2,1,0:T(8,128)(2,1)S(1)}, u32[]{:S(2)}, u32[]{:S(2)}) collective-permute-start(bf16[6,48,1024]{2,1,0:T(8,128)(2,1)S(1)} %get-tuple-element.58), channel_id=1, source_target_pairs={{1,0},{2,1},{3,2},{5,4},{6,5},{7,6},{9,8},{10,9},{11,10},{13,12},{... | collective-permute-start | bytes 1769480 | tf_op jit(solution)/shard_map/ppermute | solution.py:487
  47.4 0.0 collective-permute-done.8.refs_3_
  47.4 0.0 collective-permute-done.7.refs_2_
  47.5 0.0 collective-permute-done.6.refs_1_
  47.5 1.6 %project.3 = (f32[8,64,1024]{2,1,0:T(8,128)S(1)}, bf16[6,64,1024]{2,1,0:T(8,128)(2,1)S(1)}, bf16[6,64,1024]{2,1,0:T(8,128)(2,1)S(1)}, f32[8,128]{1,0:T(8,128)S(1)}) custom-call(f32[64,512]{1,0:T(8,128)S(1)} %get-tuple-element.49.refs_0_, bf16[64,512]{1,0:T(8,128)(2,1)S(1)} %collective-permute-done.6.refs_1_, ...), custom_call_target="tpu_custom_call" | custom-call | flops 1000000000 | bytes 1024 | tf_op jit(solution)/shard_map/project/pallas_call | solution.py:71
  49.0 3.3 %collective-permute-start.9 = (bf16[6,64,1024]{2,1,0:T(8,128)(2,1)S(1)}, bf16[6,64,1024]{2,1,0:T(8,128)(2,1)S(1)}, u32[]{:S(2)}, u32[]{:S(2)}) collective-permute-start(bf16[6,64,1024]{2,1,0:T(8,128)(2,1)S(1)} %get-tuple-element.54), channel_id=1, source_target_pairs={{0,1},{1,2},{2,3},{4,5},{5,6},{6,7},{8,9},{9,10},{10,11},{12,13},{... | collective-permute-start | bytes 2359304 | tf_op jit(solution)/shard_map/ppermute | solution.py:491
  52.4 1.3 %collective-permute-start.10 = (bf16[6,64,1024]{2,1,0:T(8,128)(2,1)S(1)}, bf16[6,64,1024]{2,1,0:T(8,128)(2,1)S(1)}, u32[]{:S(2)}, u32[]{:S(2)}) collective-permute-start(bf16[6,64,1024]{2,1,0:T(8,128)(2,1)S(1)} %get-tuple-element.55), channel_id=1, source_target_pairs={{1,0},{2,1},{3,2},{5,4},{6,5},{7,6},{9,8},{10,9},{11,10},{13,12},{... | collective-permute-start | bytes 2359304 | tf_op jit(solution)/shard_map/ppermute | solution.py:491
  53.7 0.0 collective-permute-done.11.refs_1_
  53.7 0.0 collective-permute-done.12.refs_2_
  53.7 5.2 %filter_ahead.1 = (f32[20,1024]{1,0:T(8,128)S(1)}, f32[20,1024]{1,0:T(8,128)S(1)}, f32[2,8,128]{2,1,0:T(8,128)S(1)}, f32[8,32,1024]{2,1,0:T(8,128)S(1)}, f32[8,128]{1,0:T(8,128)S(1)}) custom-call(f32[8,32,1024]{2,1,0:T(8,128)S(1)} %get-tuple-element.56.refs_0_, bf16[6,48,1024]{2,1,0:T(8,128)(2,1)S(1)} %collective-permute-done.11.refs_1_, ...), custom_call_target="tpu_custom_call" | custom-call | flops 3500000000 | bytes 1024 | tf_op jit(solution)/shard_map/filter_ahead/pallas_call | solution.py:71
  58.9 0.0 collective-permute-done.9.refs_1_
  58.9 0.0 collective-permute-done.10.refs_2_
  59.0 13.4 %filter_rest.1 = (f32[8,64,1024]{2,1,0:T(8,128)S(1)}, f32[96,512]{1,0:T(8,128)S(1)}, bf16[96,512]{1,0:T(8,128)(2,1)S(1)}, f32[8,128]{1,0:T(8,128)S(1)}) custom-call(f32[8,64,1024]{2,1,0:T(8,128)S(1)} %get-tuple-element.53.refs_0_, bf16[6,64,1024]{2,1,0:T(8,128)(2,1)S(1)} %collective-permute-done.9.refs_1_, ...), custom_call_target="tpu_custom_call" | custom-call | flops 7000000000 | bytes 1024 | tf_op jit(solution)/shard_map/filter_rest/pallas_call | solution.py:71
  72.4 2.4 %collective-permute-start.15 = (bf16[96,512]{1,0:T(8,128)(2,1)S(1)}, bf16[96,512]{1,0:T(8,128)(2,1)S(1)}, u32[]{:S(2)}, u32[]{:S(2)}) collective-permute-start(bf16[96,512]{1,0:T(8,128)(2,1)S(1)} %get-tuple-element.66), channel_id=1, source_target_pairs={{0,3},{1,2},{2,1},{3,0},{4,7},{5,6},{6,5},{7,4},{8,11},{9,10},{10,... | collective-permute-start | bytes 294920 | tf_op jit(solution)/shard_map/ppermute | solution.py:256
  74.9 7.7 %collective-permute-start.14 = (bf16[96,512]{1,0:T(8,128)(2,1)S(1)}, bf16[96,512]{1,0:T(8,128)(2,1)S(1)}, u32[]{:S(2)}, u32[]{:S(2)}) collective-permute-start(bf16[96,512]{1,0:T(8,128)(2,1)S(1)} %get-tuple-element.66), channel_id=1, source_target_pairs={{0,2},{1,3},{2,0},{3,1},{4,6},{5,7},{6,4},{7,5},{8,10},{9,11},{10,... | collective-permute-start | bytes 294920 | tf_op jit(solution)/shard_map/ppermute | solution.py:256
  82.6 0.0 collective-permute-start.13
  82.6 0.0 collective-permute-done.15.refs_3_
  82.6 4.2 %collective-permute-done.14.refs_2_ = bf16[96,512]{1,0:T(8,128)(2,1)S(1)} collective-permute-done((bf16[96,512]{1,0:T(8,128)(2,1)S(1)}, bf16[96,512]{1,0:T(8,128)(2,1)S(1)}, u32[]{:S(2)}, u32[]{:S(2)}) %collective-permute-start.14) | collective-permute-done | bytes 98336 | tf_op jit(solution)/shard_map/ppermute | solution.py:256
  86.8 0.0 collective-permute-done.13.refs_1_
  86.8 4.2 %clean.1 = (f32[256,1024]{1,0:T(8,128)}, f32[8,1024]{1,0:T(8,128)}, f32[8,128]{1,0:T(8,128)}) custom-call(f32[96,512]{1,0:T(8,128)S(1)} %get-tuple-element.65.refs_0_, bf16[96,512]{1,0:T(8,128)(2,1)S(1)} %collective-permute-done.13.refs_1_, bf16[96,512]{1,0:T(8,128)(2,1)S(1)} %collective-permute-done.14.refs_2_, ...), custom_call_target="tpu_custom_call" | custom-call | flops 2000000000 | bytes 1024 | tf_op jit(solution)/shard_map/clean/pallas_call | solution.py:71
Async XLA Ops:
  0.6 28.6 %collective-permute-start = (bf16[32,8,1024]{2,1,0:T(8,128)(2,1)}, bf16[32,8,1024]{2,1,0:T(8,128)(2,1)S(1)}, u32[]{:S(2)}, u32[]{:S(2)}) collective-permute-start(bf16[32,8,1024]{2,1,0:T(8,128)(2,1)} %param.4), channel_id=1, source_target_pairs={{0,8},{4,12},{8,16},{12,20},{16,24},{20,28},{24,32},{28,36},{32,40... | collective-permute-start | bytes 1572872 | tf_op jit(solution)/shard_map/ppermute | solution.py:470
  2.7 17.0 %collective-permute-start.1 = (bf16[32,8,1024]{2,1,0:T(8,128)(2,1)}, bf16[32,8,1024]{2,1,0:T(8,128)(2,1)S(1)}, u32[]{:S(2)}, u32[]{:S(2)}) collective-permute-start(bf16[32,8,1024]{2,1,0:T(8,128)(2,1)} %param.4), channel_id=1, source_target_pairs={{0,4},{4,0},{8,12},{12,8},{16,20},{20,16},{24,28},{28,24},{32,36},... | collective-permute-start | bytes 1572872 | tf_op jit(solution)/shard_map/ppermute | solution.py:470
  5.9 8.7 %copy-start.1 = (f32[1,8,1024]{2,1,0:T(8,128)S(1)}, f32[1,8,1024]{2,1,0:T(8,128)}, u32[]{:S(2)}) copy-start(f32[1,8,1024]{2,1,0:T(8,128)} %param.7) | copy-start | bytes 98308
  5.9 8.7 %copy-start.2 = (s32[1,1024]{1,0:T(1,128)S(1)}, s32[1,1024]{1,0:T(1,128)}, u32[]{:S(2)}) copy-start(s32[1,1024]{1,0:T(1,128)} %refs_0_.1) | copy-start | bytes 12292
  14.6 1.9 %copy-start = (bf16[32,8,1024]{2,1,0:T(8,128)(2,1)S(1)}, bf16[32,8,1024]{2,1,0:T(8,128)(2,1)}, u32[]{:S(2)}) copy-start(bf16[32,8,1024]{2,1,0:T(8,128)(2,1)} %param.4) | copy-start | bytes 1572868
  19.7 18.3 %collective-permute-start.2 = (bf16[32,8,1024]{2,1,0:T(8,128)(2,1)S(1)}, bf16[32,8,1024]{2,1,0:T(8,128)(2,1)S(1)}, u32[]{:S(2)}, u32[]{:S(2)}) collective-permute-start(bf16[32,8,1024]{2,1,0:T(8,128)(2,1)S(1)} %collective-permute-done.1), channel_id=1, source_target_pairs={{0,8},{8,16},{16,24},{24,32},{32,40},{40,48},{48,56},{56,64},{64,7... | collective-permute-start | bytes 1572872 | tf_op jit(solution)/shard_map/ppermute | solution.py:470
  23.5 3.4 %collective-permute-start.5 = (bf16[32,512]{1,0:T(8,128)(2,1)S(1)}, bf16[32,512]{1,0:T(8,128)(2,1)S(1)}, u32[]{:S(2)}, u32[]{:S(2)}) collective-permute-start(bf16[32,512]{1,0:T(8,128)(2,1)S(1)} %get-tuple-element.44), channel_id=1, source_target_pairs={{0,3},{1,2},{2,1},{3,0},{4,7},{5,6},{6,5},{7,4},{8,11},{9,10},{10,... | collective-permute-start | bytes 98312 | tf_op jit(solution)/shard_map/ppermute | solution.py:256
  23.6 4.1 %collective-permute-start.4 = (bf16[32,512]{1,0:T(8,128)(2,1)S(1)}, bf16[32,512]{1,0:T(8,128)(2,1)S(1)}, u32[]{:S(2)}, u32[]{:S(2)}) collective-permute-start(bf16[32,512]{1,0:T(8,128)(2,1)S(1)} %get-tuple-element.44), channel_id=1, source_target_pairs={{0,2},{1,3},{2,0},{3,1},{4,6},{5,7},{6,4},{7,5},{8,10},{9,11},{10,... | collective-permute-start | bytes 98312 | tf_op jit(solution)/shard_map/ppermute | solution.py:256
  24.4 3.3 %collective-permute-start.3 = (bf16[32,512]{1,0:T(8,128)(2,1)S(1)}, bf16[32,512]{1,0:T(8,128)(2,1)S(1)}, u32[]{:S(2)}, u32[]{:S(2)}) collective-permute-start(bf16[32,512]{1,0:T(8,128)(2,1)S(1)} %get-tuple-element.44), channel_id=1, source_target_pairs={{0,1},{1,0},{2,3},{3,2},{4,5},{5,4},{6,7},{7,6},{8,9},{9,8},{10,11... | collective-permute-start | bytes 98312 | tf_op jit(solution)/shard_map/ppermute | solution.py:256
  42.1 5.4 %collective-permute-start.8 = (bf16[64,512]{1,0:T(8,128)(2,1)S(1)}, bf16[64,512]{1,0:T(8,128)(2,1)S(1)}, u32[]{:S(2)}, u32[]{:S(2)}) collective-permute-start(bf16[64,512]{1,0:T(8,128)(2,1)S(1)} %get-tuple-element.50), channel_id=1, source_target_pairs={{0,3},{1,2},{2,1},{3,0},{4,7},{5,6},{6,5},{7,4},{8,11},{9,10},{10,... | collective-permute-start | bytes 196616 | tf_op jit(solution)/shard_map/ppermute | solution.py:256
  42.2 5.3 %collective-permute-start.7 = (bf16[64,512]{1,0:T(8,128)(2,1)S(1)}, bf16[64,512]{1,0:T(8,128)(2,1)S(1)}, u32[]{:S(2)}, u32[]{:S(2)}) collective-permute-start(bf16[64,512]{1,0:T(8,128)(2,1)S(1)} %get-tuple-element.50), channel_id=1, source_target_pairs={{0,2},{1,3},{2,0},{3,1},{4,6},{5,7},{6,4},{7,5},{8,10},{9,11},{10,... | collective-permute-start | bytes 196616 | tf_op jit(solution)/shard_map/ppermute | solution.py:256
  42.9 4.5 %collective-permute-start.6 = (bf16[64,512]{1,0:T(8,128)(2,1)S(1)}, bf16[64,512]{1,0:T(8,128)(2,1)S(1)}, u32[]{:S(2)}, u32[]{:S(2)}) collective-permute-start(bf16[64,512]{1,0:T(8,128)(2,1)S(1)} %get-tuple-element.50), channel_id=1, source_target_pairs={{0,1},{1,0},{2,3},{3,2},{4,5},{5,4},{6,7},{7,6},{8,9},{9,8},{10,11... | collective-permute-start | bytes 196616 | tf_op jit(solution)/shard_map/ppermute | solution.py:256
  44.0 9.7 %collective-permute-start.11 = (bf16[6,48,1024]{2,1,0:T(8,128)(2,1)S(1)}, bf16[6,48,1024]{2,1,0:T(8,128)(2,1)S(1)}, u32[]{:S(2)}, u32[]{:S(2)}) collective-permute-start(bf16[6,48,1024]{2,1,0:T(8,128)(2,1)S(1)} %get-tuple-element.57), channel_id=1, source_target_pairs={{0,1},{1,2},{2,3},{4,5},{5,6},{6,7},{8,9},{9,10},{10,11},{12,13},{... | collective-permute-start | bytes 1769480 | tf_op jit(solution)/shard_map/ppermute | solution.py:487
  46.0 7.8 %collective-permute-start.12 = (bf16[6,48,1024]{2,1,0:T(8,128)(2,1)S(1)}, bf16[6,48,1024]{2,1,0:T(8,128)(2,1)S(1)}, u32[]{:S(2)}, u32[]{:S(2)}) collective-permute-start(bf16[6,48,1024]{2,1,0:T(8,128)(2,1)S(1)} %get-tuple-element.58), channel_id=1, source_target_pairs={{1,0},{2,1},{3,2},{5,4},{6,5},{7,6},{9,8},{10,9},{11,10},{13,12},{... | collective-permute-start | bytes 1769480 | tf_op jit(solution)/shard_map/ppermute | solution.py:487
  49.0 9.9 %collective-permute-start.9 = (bf16[6,64,1024]{2,1,0:T(8,128)(2,1)S(1)}, bf16[6,64,1024]{2,1,0:T(8,128)(2,1)S(1)}, u32[]{:S(2)}, u32[]{:S(2)}) collective-permute-start(bf16[6,64,1024]{2,1,0:T(8,128)(2,1)S(1)} %get-tuple-element.54), channel_id=1, source_target_pairs={{0,1},{1,2},{2,3},{4,5},{5,6},{6,7},{8,9},{9,10},{10,11},{12,13},{... | collective-permute-start | bytes 2359304 | tf_op jit(solution)/shard_map/ppermute | solution.py:491
  52.4 6.6 %collective-permute-start.10 = (bf16[6,64,1024]{2,1,0:T(8,128)(2,1)S(1)}, bf16[6,64,1024]{2,1,0:T(8,128)(2,1)S(1)}, u32[]{:S(2)}, u32[]{:S(2)}) collective-permute-start(bf16[6,64,1024]{2,1,0:T(8,128)(2,1)S(1)} %get-tuple-element.55), channel_id=1, source_target_pairs={{1,0},{2,1},{3,2},{5,4},{6,5},{7,6},{9,8},{10,9},{11,10},{13,12},{... | collective-permute-start | bytes 2359304 | tf_op jit(solution)/shard_map/ppermute | solution.py:491
  72.4 10.1 %collective-permute-start.15 = (bf16[96,512]{1,0:T(8,128)(2,1)S(1)}, bf16[96,512]{1,0:T(8,128)(2,1)S(1)}, u32[]{:S(2)}, u32[]{:S(2)}) collective-permute-start(bf16[96,512]{1,0:T(8,128)(2,1)S(1)} %get-tuple-element.66), channel_id=1, source_target_pairs={{0,3},{1,2},{2,1},{3,0},{4,7},{5,6},{6,5},{7,4},{8,11},{9,10},{10,... | collective-permute-start | bytes 294920 | tf_op jit(solution)/shard_map/ppermute | solution.py:256
  74.9 11.9 %collective-permute-start.14 = (bf16[96,512]{1,0:T(8,128)(2,1)S(1)}, bf16[96,512]{1,0:T(8,128)(2,1)S(1)}, u32[]{:S(2)}, u32[]{:S(2)}) collective-permute-start(bf16[96,512]{1,0:T(8,128)(2,1)S(1)} %get-tuple-element.66), channel_id=1, source_target_pairs={{0,2},{1,3},{2,0},{3,1},{4,6},{5,7},{6,4},{7,5},{8,10},{9,11},{10,... | collective-permute-start | bytes 294920 | tf_op jit(solution)/shard_map/ppermute | solution.py:256
  82.6 4.2 %collective-permute-start.13 = (bf16[96,512]{1,0:T(8,128)(2,1)S(1)}, bf16[96,512]{1,0:T(8,128)(2,1)S(1)}, u32[]{:S(2)}, u32[]{:S(2)}) collective-permute-start(bf16[96,512]{1,0:T(8,128)(2,1)S(1)} %get-tuple-element.66), channel_id=1, source_target_pairs={{0,1},{1,0},{2,3},{3,2},{4,5},{5,4},{6,7},{7,6},{8,9},{9,8},{10,11... | collective-permute-start | bytes 294920 | tf_op jit(solution)/shard_map/ppermute | solution.py:256

commit v3 on v2

--- a/solution.py
+++ b/solution.py
@@ -6,6 +6,7 @@
 from jax.experimental import pallas as pl
 from jax.experimental.pallas import tpu as pltpu
 from jax.sharding import PartitionSpec as P
+
 
 BZ = 32
 KDEG = 6
@@ -45,6 +46,7 @@
 ANY = pl.BlockSpec(memory_space=pl.ANY)
 MIB = 1 << 20
 PIECE = 32
+SCALE = 500e6
 CHUNKS = NCORE // PIECE
 NT = (((1,), (1,)), ((), ()))
 
@@ -53,7 +55,7 @@
     def __init__(self):
         self.token = None
 
-    def call(self, kernel, name, out_shape, args, specs=None, scratch=(), limit=8, micros=2):
+    def call(self, kernel, out_shape, args, specs=None, scratch=(), limit=8, micros=2):
         specs = list(specs or [VMEM] * len(args))
         args = list(args)
         waits = self.token is not None
@@ -76,9 +78,8 @@
             scratch_shapes=list(scratch),
             compiler_params=pltpu.CompilerParams(vmem_limit_bytes=limit * MIB),
             cost_estimate=pl.CostEstimate(
-                flops=int(micros * 500e6), bytes_accessed=1024, transcendentals=0
+                flops=int(micros * SCALE), bytes_accessed=1024, transcendentals=0
             ),
-            name=name,
         )(*args)
         self.token = got[-1]
         return got[:-1]
@@ -137,11 +138,7 @@
 def prepare(line, plane_map, local):
     square = struct((PLANE, PLANE), BF16)
     return line.call(
-        prepare_kernel,
-        "prepare",
-        (square, square, struct((SLAB, PLANE), F32)),
-        (plane_map, local),
-        micros=2,
+        prepare_kernel, (square, square, struct((SLAB, PLANE), F32)), (plane_map, local), micros=2
     )
 
 
@@ -149,7 +146,7 @@
     def fetch(i):
         return pltpu.make_async_copy(core_hbm.at[pl.ds(i * 256, 256), :], raw.at[i], sems.at[i])
 
-    for i in range(CHUNKS):
+    for i in range(8):
         fetch(i).start()
     rows_ref[...] = row_permutation(256, SLAB)
     src, out = iota((256, 256), 0), iota((256, 256), 1)
@@ -185,6 +182,11 @@
 
     @pl.loop(0, CHUNKS // 4)
     def _(i):
+        @pl.when(i < CHUNKS // 4 - 2)
+        def _():
+            for k in range(4):
+                fetch(4 * i + 8 + k).start()
+
         for k in range(4):
             fetch(4 * i + k).wait()
         for k in range(5):
@@ -198,7 +200,6 @@
     square = pltpu.VMEM((256, 256), BF16)
     return line.call(
         relayout_kernel,
-        "relayout",
         (struct((SLAB, NCORE, PLANE), BF16),),
         (core.reshape(NCORE * SLAB, PLANE),),
         specs=[pl.BlockSpec(memory_space=pltpu.HBM)],
@@ -244,7 +245,6 @@
     flat = [a.reshape(BATCH * SLAB, PLANE) for b in batches for a in b]
     return line.call(
         lambda *refs: map_kernel(counts, *refs),
-        "map_batches",
         (struct((SLAB, rows, PLANE), BF16), struct((rows, NCORE), F32), struct((rows, NCORE), BF16)),
         (pick, core_x, *flat),
         micros=2 + len(batches) // 2,
@@ -265,7 +265,6 @@
 def project_kernel(full_ref, a_ref, b_ref, c_ref, field_ref, core_ref, *refs):
     local_ref = refs[0] if len(refs) == 4 else None
     out_ref, low_ref, high_ref = refs[-3:]
-    rows = field_ref.shape[1]
     coef = total_of(full_ref, a_ref, b_ref, c_ref)
     for x in range(SLAB):
         value = field_ref[x].astype(F32) - dot(coef, core_ref[x])
@@ -287,7 +286,6 @@
     sent = rows + (16 if local is not None else 0)
     return line.call(
         project_kernel,
-        "project",
         (
             struct((SLAB, rows, PLANE), F32),
             struct((HALO, sent, PLANE), BF16),
@@ -407,7 +405,6 @@
     wide = struct((WIDE, PLANE), F32)
     got = line.call(
         lambda *refs: filter_kernel(True, *refs),
-        "filter_ahead",
         (wide, wide, struct((2, 8, LANES), F32), struct((SLAB, rows, PLANE), F32)),
         (field, below, above, local),
         scratch=filter_scratch(),
@@ -421,7 +418,6 @@
     total = rows + ahead.shape[1]
     return line.call(
         lambda *refs: filter_kernel(False, *refs),
-        "filter_rest",
         (struct((SLAB, rows, PLANE), F32), struct((total, NCORE), F32), struct((total, NCORE), BF16)),
         (field, below, above, *weight, core_x, ahead),
         scratch=filter_scratch(),
@@ -457,7 +453,6 @@
     small, own = struct((SLAB, PLANE), F32), struct((SLAB * BATCH, PLANE), F32)
     return line.call(
         clean_kernel,
-        "clean",
         (own, small),
         (full, *others, ahead, rest, mapped, mapped_rest, core_x, order),
         scratch=[pltpu.VMEM(own.shape, F32), pltpu.VMEM(small.shape, F32)],
@@ -479,14 +474,16 @@
     core_x = relayout(line, core_orbitals[0])
     order, pick, local = prepare(line, plane_map, potential[0])
 
+    mate, line.token = lax.optimization_barrier((mate, line.token))
+    second = permute_groups(mate, [(i, (i + 2) % groups) for i in range(0, groups, 2)])
     mapped, full, half = map_batches(line, pick, core_x, [(stochastic,)])
     others = exchange(half)
-    mate, line.token = lax.optimization_barrier((mate, line.token))
-    second = permute_groups(mate, [(i, (i + 2) % groups) for i in range(0, groups, 2)])
     field, low, high = project(line, full, others, mapped, core_x, local)
-    below, above = lax.ppermute(high, "grid", UP), lax.ppermute(low, "grid", DOWN)
-
-    mapped_rest, full, half = map_batches(line, pick, core_x, [(third,), (mate, second)])
+    below = lax.ppermute(high, "grid", UP)
+    above = lax.ppermute(low, "grid", DOWN)
+
+    batches = [(third,), (mate, second)]
+    mapped_rest, full, half = map_batches(line, pick, core_x, batches)
     rest, low, high = project(line, full, exchange(half), mapped_rest, core_x, None)
     below_rest, above_rest = lax.ppermute(high, "grid", UP), lax.ppermute(low, "grid", DOWN)
 

time: 91.2 us -> 90.1 us (0.988)
  waiting for transfers between devices: 15.2 us -> 12.8 us
  Pallas kernels: 43.8 us -> 44.8 us
    ppermute x0 -> x2, starting transfers between devices: none -> 3.71 us  [the longest x1 2.24 us: body(): below = lax.ppermute(high, 'grid', UP)]
    ppermute x3, waiting for transfers between devices: 8.75 us -> 6.22 us  [permute_groups(): return lax.ppermute(array, 'group', pairs)]
    ppermute x2 -> x1, starting transfers between devices: 5.27 us -> 3.75 us  [body(): lax.ppermute(high, 'grid', UP)]
    ppermute x2 -> x1, starting transfers between devices: 2.76 us -> 1.29 us  [body(): lax.ppermute(low, 'grid', DOWN)]
    pallas_call x9, Pallas kernels: 43.8 us -> 44.8 us  [call(): pl.pallas_call(with_token, in_specs=specs, out_specs=tuple((VMEM for _ in...]
  transfers between devices with their start and end apart: 16 -> 16, of which waited for: 4 -> 5; matrix products, arithmetic and copies ran while one was open for 0% -> 0% of each run, Pallas kernels for 24% -> 25%
where the time goes in v3:
time: 90.1 us; the launch traced here: 89.9 us
  Pallas kernels  44.8 us (50%)
  starting transfers between devices  31.5 us (35%)
  waiting for transfers between devices  12.8 us (14%)
    pallas_call x9, Pallas kernels, call(): pl.pallas_call(with_token, in_specs=specs, out_specs=tuple((VMEM for _ in...  44.8 us
    ppermute x9, starting transfers between devices, exchange(): lax.ppermute(half, 'grid', [(i, i ^ k) for i in range(GRID)])  13.6 us
    ppermute x3, starting transfers between devices, permute_groups(): return lax.ppermute(array, 'group', pairs)  9.13 us
    ppermute x9, waiting for transfers between devices, exchange(): lax.ppermute(half, 'grid', [(i, i ^ k) for i in range(GRID)])  6.56 us
    ppermute x3, waiting for transfers between devices, permute_groups(): return lax.ppermute(array, 'group', pairs)  6.22 us
    ppermute x1, starting transfers between devices, body(): lax.ppermute(high, 'grid', UP)  3.75 us
    ppermute x1, starting transfers between devices, body(): below = lax.ppermute(high, 'grid', UP)  2.24 us
  transfers between devices with their start and end apart: 16, of which 5 were waited for; matrix products, arithmetic and copies ran while one was open for 0% of the time, Pallas kernels for 25%

profile of v3, /device:TPU:0, one launch (start us, length us, event | category | flops | bytes accessed | tf_op | source)
XLA Modules:
  0.0 89.9 jit_solution(18145464901671208849)
XLA Ops:
  0.6 3.4 %collective-permute-start.1 = (bf16[32,8,1024]{2,1,0:T(8,128)(2,1)}, bf16[32,8,1024]{2,1,0:T(8,128)(2,1)S(1)}, u32[]{:S(2)}, u32[]{:S(2)}) collective-permute-start(bf16[32,8,1024]{2,1,0:T(8,128)(2,1)} %param.4), channel_id=1, source_target_pairs={{0,4},{4,0},{8,12},{12,8},{16,20},{20,16},{24,28},{28,24},{32,36},... | collective-permute-start | bytes 1572872 | tf_op jit(solution)/shard_map/ppermute | solution.py:465
  4.0 1.9 %collective-permute-start = (bf16[32,8,1024]{2,1,0:T(8,128)(2,1)}, bf16[32,8,1024]{2,1,0:T(8,128)(2,1)S(1)}, u32[]{:S(2)}, u32[]{:S(2)}) collective-permute-start(bf16[32,8,1024]{2,1,0:T(8,128)(2,1)} %param.4), channel_id=1, source_target_pairs={{0,8},{4,12},{8,16},{12,20},{16,24},{20,28},{24,32},{28,36},{32,40... | collective-permute-start | bytes 1572872 | tf_op jit(solution)/shard_map/ppermute | solution.py:465
  5.9 0.0 copy-start.1
  5.9 0.0 copy-start.2
  5.9 8.6 %shard_map.59 = (bf16[8,512,1024]{2,1,0:T(8,128)(2,1)S(1)}, f32[8,128]{1,0:T(8,128)S(1)}) custom-call(bf16[4096,1024]{1,0:T(8,128)(2,1)} %bitcast.13), custom_call_target="tpu_custom_call" | custom-call | flops 4000000000 | bytes 1024 | tf_op jit(solution)/shard_map/pallas_call | solution.py:73
  14.6 0.0 copy-start
  14.6 0.0 copy-done.1
  14.6 0.0 copy-done.2
  14.6 1.8 %shard_map.60 = (bf16[1024,1024]{1,0:T(8,128)(2,1)S(1)}, bf16[1024,1024]{1,0:T(8,128)(2,1)S(1)}, f32[8,1024]{1,0:T(8,128)S(1)}, f32[8,128]{1,0:T(8,128)S(1)}) custom-call(s32[1,1024]{1,0:T(1,128)S(1)} %copy-done.2, f32[8,1024]{1,0:T(8,128)S(1)} %bitcast.12, f32[8,128]{1,0:T(8,128)S(1)} %get-tuple-element.37.refs_2_), custom_call_target="tpu_custom_call" | custom-call | flops 1000000000 | bytes 1024 | tf_op jit(solution)/shard_map/pallas_call | solution.py:73
  16.4 0.0 collective-permute-done.1
  16.5 3.8 %collective-permute-start.2 = (bf16[32,8,1024]{2,1,0:T(8,128)(2,1)S(1)}, bf16[32,8,1024]{2,1,0:T(8,128)(2,1)S(1)}, u32[]{:S(2)}, u32[]{:S(2)}) collective-permute-start(bf16[32,8,1024]{2,1,0:T(8,128)(2,1)S(1)} %collective-permute-done.1), channel_id=1, source_target_pairs={{0,8},{8,16},{16,24},{24,32},{32,40},{40,48},{48,56},{56,64},{64,7... | collective-permute-start | bytes 1572872 | tf_op jit(solution)/shard_map/ppermute | solution.py:465
  20.3 0.0 copy-done
  20.3 3.2 %shard_map.61 = (bf16[8,32,1024]{2,1,0:T(8,128)(2,1)S(1)}, f32[32,512]{1,0:T(8,128)S(1)}, bf16[32,512]{1,0:T(8,128)(2,1)S(1)}, f32[8,128]{1,0:T(8,128)S(1)}) custom-call(bf16[1024,1024]{1,0:T(8,128)(2,1)S(1)} %get-tuple-element.38.refs_0_, bf16[8,512,1024]{2,1,0:T(8,128)(2,1)S(1)} %get-tuple-element.39.refs_1_.refs_5_.refs_6_.refs_8_, ...), custom_call_target="tpu_custom_call" | custom-call | flops 1000000000 | bytes 1024 | tf_op jit(solution)/shard_map/pallas_call | solution.py:73
  23.5 0.0 collective-permute-start.5
  23.6 1.4 %collective-permute-start.4 = (bf16[32,512]{1,0:T(8,128)(2,1)S(1)}, bf16[32,512]{1,0:T(8,128)(2,1)S(1)}, u32[]{:S(2)}, u32[]{:S(2)}) collective-permute-start(bf16[32,512]{1,0:T(8,128)(2,1)S(1)} %get-tuple-element.44), channel_id=1, source_target_pairs={{0,2},{1,3},{2,0},{3,1},{4,6},{5,7},{6,4},{7,5},{8,10},{9,11},{10,... | collective-permute-start | bytes 98312 | tf_op jit(solution)/shard_map/ppermute | solution.py:256
  25.0 0.5 collective-permute-start.3
  25.4 1.7 %collective-permute-done.5.refs_3_ = bf16[32,512]{1,0:T(8,128)(2,1)S(1)} collective-permute-done((bf16[32,512]{1,0:T(8,128)(2,1)S(1)}, bf16[32,512]{1,0:T(8,128)(2,1)S(1)}, u32[]{:S(2)}, u32[]{:S(2)}) %collective-permute-start.5) | collective-permute-done | bytes 32800 | tf_op jit(solution)/shard_map/ppermute | solution.py:256
  27.1 0.4 collective-permute-done.4.refs_2_
  27.6 0.0 collective-permute-done.3.refs_1_
  27.6 1.6 %shard_map.62 = (f32[8,32,1024]{2,1,0:T(8,128)S(1)}, bf16[6,48,1024]{2,1,0:T(8,128)(2,1)S(1)}, bf16[6,48,1024]{2,1,0:T(8,128)(2,1)S(1)}, f32[8,128]{1,0:T(8,128)S(1)}) custom-call(f32[32,512]{1,0:T(8,128)S(1)} %get-tuple-element.43.refs_0_, bf16[32,512]{1,0:T(8,128)(2,1)S(1)} %collective-permute-done.3.refs_1_, ...), custom_call_target="tpu_custom_call" | custom-call | flops 1000000000 | bytes 1024 | tf_op jit(solution)/shard_map/pallas_call | solution.py:73
  29.2 0.0 collective-permute-done
  29.2 6.2 %collective-permute-done.2 = bf16[32,8,1024]{2,1,0:T(8,128)(2,1)S(1)} collective-permute-done((bf16[32,8,1024]{2,1,0:T(8,128)(2,1)S(1)}, bf16[32,8,1024]{2,1,0:T(8,128)(2,1)S(1)}, u32[]{:S(2)}, u32[]{:S(2)}) %collective-permute-start.2) | collective-permute-done | bytes 524320 | tf_op jit(solution)/shard_map/ppermute | solution.py:465
  35.4 4.1 %shard_map.63 = (bf16[8,64,1024]{2,1,0:T(8,128)(2,1)S(1)}, f32[64,512]{1,0:T(8,128)S(1)}, bf16[64,512]{1,0:T(8,128)(2,1)S(1)}, f32[8,128]{1,0:T(8,128)S(1)}) custom-call(bf16[1024,1024]{1,0:T(8,128)(2,1)S(1)} %get-tuple-element.38.refs_0_, bf16[8,512,1024]{2,1,0:T(8,128)(2,1)S(1)} %get-tuple-element.39.refs_1_.refs_5_.refs_6_.refs_8_, ...), custom_call_target="tpu_custom_call" | custom-call | flops 1500000000 | bytes 1024 | tf_op jit(solution)/shard_map/pallas_call | solution.py:73
  39.5 0.1 collective-permute-start.8
  39.5 1.6 %collective-permute-start.7 = (bf16[64,512]{1,0:T(8,128)(2,1)S(1)}, bf16[64,512]{1,0:T(8,128)(2,1)S(1)}, u32[]{:S(2)}, u32[]{:S(2)}) collective-permute-start(bf16[64,512]{1,0:T(8,128)(2,1)S(1)} %get-tuple-element.50), channel_id=1, source_target_pairs={{0,2},{1,3},{2,0},{3,1},{4,6},{5,7},{6,4},{7,5},{8,10},{9,11},{10,... | collective-permute-start | bytes 196616 | tf_op jit(solution)/shard_map/ppermute | solution.py:256
  41.2 0.2 collective-permute-start.6
  41.4 2.2 %collective-permute-start.11 = (bf16[6,48,1024]{2,1,0:T(8,128)(2,1)S(1)}, bf16[6,48,1024]{2,1,0:T(8,128)(2,1)S(1)}, u32[]{:S(2)}, u32[]{:S(2)}) collective-permute-start(bf16[6,48,1024]{2,1,0:T(8,128)(2,1)S(1)} %get-tuple-element.57), channel_id=1, source_target_pairs={{0,1},{1,2},{2,3},{4,5},{5,6},{6,7},{8,9},{9,10},{10,11},{12,13},{... | collective-permute-start | bytes 1769480 | tf_op jit(solution)/shard_map/ppermute | solution.py:482
  43.6 1.5 %collective-permute-start.12 = (bf16[6,48,1024]{2,1,0:T(8,128)(2,1)S(1)}, bf16[6,48,1024]{2,1,0:T(8,128)(2,1)S(1)}, u32[]{:S(2)}, u32[]{:S(2)}) collective-permute-start(bf16[6,48,1024]{2,1,0:T(8,128)(2,1)S(1)} %get-tuple-element.58), channel_id=1, source_target_pairs={{1,0},{2,1},{3,2},{5,4},{6,5},{7,6},{9,8},{10,9},{11,10},{13,12},{... | collective-permute-start | bytes 1769480 | tf_op jit(solution)/shard_map/ppermute | solution.py:483
  45.1 0.0 collective-permute-done.8.refs_3_
  45.1 0.2 collective-permute-done.7.refs_2_
  45.3 0.0 collective-permute-done.6.refs_1_
  45.3 1.6 %shard_map.64 = (f32[8,64,1024]{2,1,0:T(8,128)S(1)}, bf16[6,64,1024]{2,1,0:T(8,128)(2,1)S(1)}, bf16[6,64,1024]{2,1,0:T(8,128)(2,1)S(1)}, f32[8,128]{1,0:T(8,128)S(1)}) custom-call(f32[64,512]{1,0:T(8,128)S(1)} %get-tuple-element.49.refs_0_, bf16[64,512]{1,0:T(8,128)(2,1)S(1)} %collective-permute-done.6.refs_1_, ...), custom_call_target="tpu_custom_call" | custom-call | flops 1000000000 | bytes 1024 | tf_op jit(solution)/shard_map/pallas_call | solution.py:73
  46.9 3.7 %collective-permute-start.9 = (bf16[6,64,1024]{2,1,0:T(8,128)(2,1)S(1)}, bf16[6,64,1024]{2,1,0:T(8,128)(2,1)S(1)}, u32[]{:S(2)}, u32[]{:S(2)}) collective-permute-start(bf16[6,64,1024]{2,1,0:T(8,128)(2,1)S(1)} %get-tuple-element.54), channel_id=1, source_target_pairs={{0,1},{1,2},{2,3},{4,5},{5,6},{6,7},{8,9},{9,10},{10,11},{12,13},{... | collective-permute-start | bytes 2359304 | tf_op jit(solution)/shard_map/ppermute | solution.py:488
  50.7 1.3 %collective-permute-start.10 = (bf16[6,64,1024]{2,1,0:T(8,128)(2,1)S(1)}, bf16[6,64,1024]{2,1,0:T(8,128)(2,1)S(1)}, u32[]{:S(2)}, u32[]{:S(2)}) collective-permute-start(bf16[6,64,1024]{2,1,0:T(8,128)(2,1)S(1)} %get-tuple-element.55), channel_id=1, source_target_pairs={{1,0},{2,1},{3,2},{5,4},{6,5},{7,6},{9,8},{10,9},{11,10},{13,12},{... | collective-permute-start | bytes 2359304 | tf_op jit(solution)/shard_map/ppermute | solution.py:488
  52.0 0.0 collective-permute-done.11.refs_1_
  52.0 0.0 collective-permute-done.12.refs_2_
  52.0 5.6 %shard_map.65 = (f32[20,1024]{1,0:T(8,128)S(1)}, f32[20,1024]{1,0:T(8,128)S(1)}, f32[2,8,128]{2,1,0:T(8,128)S(1)}, f32[8,32,1024]{2,1,0:T(8,128)S(1)}, f32[8,128]{1,0:T(8,128)S(1)}) custom-call(f32[8,32,1024]{2,1,0:T(8,128)S(1)} %get-tuple-element.56.refs_0_, bf16[6,48,1024]{2,1,0:T(8,128)(2,1)S(1)} %collective-permute-done.11.refs_1_, ...), custom_call_target="tpu_custom_call" | custom-call | flops 3500000000 | bytes 1024 | tf_op jit(solution)/shard_map/pallas_call | solution.py:73
  57.6 0.0 collective-permute-done.9.refs_1_
  57.6 0.0 collective-permute-done.10.refs_2_
  57.6 14.1 %shard_map.66 = (f32[8,64,1024]{2,1,0:T(8,128)S(1)}, f32[96,512]{1,0:T(8,128)S(1)}, bf16[96,512]{1,0:T(8,128)(2,1)S(1)}, f32[8,128]{1,0:T(8,128)S(1)}) custom-call(f32[8,64,1024]{2,1,0:T(8,128)S(1)} %get-tuple-element.53.refs_0_, bf16[6,64,1024]{2,1,0:T(8,128)(2,1)S(1)} %collective-permute-done.9.refs_1_, ...), custom_call_target="tpu_custom_call" | custom-call | flops 7000000000 | bytes 1024 | tf_op jit(solution)/shard_map/pallas_call | solution.py:73
  71.6 2.4 %collective-permute-start.15 = (bf16[96,512]{1,0:T(8,128)(2,1)S(1)}, bf16[96,512]{1,0:T(8,128)(2,1)S(1)}, u32[]{:S(2)}, u32[]{:S(2)}) collective-permute-start(bf16[96,512]{1,0:T(8,128)(2,1)S(1)} %get-tuple-element.66), channel_id=1, source_target_pairs={{0,3},{1,2},{2,1},{3,0},{4,7},{5,6},{6,5},{7,4},{8,11},{9,10},{10,... | collective-permute-start | bytes 294920 | tf_op jit(solution)/shard_map/ppermute | solution.py:256
  74.1 7.3 %collective-permute-start.14 = (bf16[96,512]{1,0:T(8,128)(2,1)S(1)}, bf16[96,512]{1,0:T(8,128)(2,1)S(1)}, u32[]{:S(2)}, u32[]{:S(2)}) collective-permute-start(bf16[96,512]{1,0:T(8,128)(2,1)S(1)} %get-tuple-element.66), channel_id=1, source_target_pairs={{0,2},{1,3},{2,0},{3,1},{4,6},{5,7},{6,4},{7,5},{8,10},{9,11},{10,... | collective-permute-start | bytes 294920 | tf_op jit(solution)/shard_map/ppermute | solution.py:256
  81.4 0.0 collective-permute-start.13
  81.4 0.0 collective-permute-done.15.refs_3_
  81.4 4.2 %collective-permute-done.14.refs_2_ = bf16[96,512]{1,0:T(8,128)(2,1)S(1)} collective-permute-done((bf16[96,512]{1,0:T(8,128)(2,1)S(1)}, bf16[96,512]{1,0:T(8,128)(2,1)S(1)}, u32[]{:S(2)}, u32[]{:S(2)}) %collective-permute-start.14) | collective-permute-done | bytes 98336 | tf_op jit(solution)/shard_map/ppermute | solution.py:256
  85.7 0.0 collective-permute-done.13.refs_1_
  85.7 4.2 %shard_map.67 = (f32[256,1024]{1,0:T(8,128)}, f32[8,1024]{1,0:T(8,128)}, f32[8,128]{1,0:T(8,128)}) custom-call(f32[96,512]{1,0:T(8,128)S(1)} %get-tuple-element.65.refs_0_, bf16[96,512]{1,0:T(8,128)(2,1)S(1)} %collective-permute-done.13.refs_1_, bf16[96,512]{1,0:T(8,128)(2,1)S(1)} %collective-permute-done.14.refs_2_, ...), custom_call_target="tpu_custom_call" | custom-call | flops 2000000000 | bytes 1024 | tf_op jit(solution)/shard_map/pallas_call | solution.py:73
Async XLA Ops:
  0.6 15.8 %collective-permute-start.1 = (bf16[32,8,1024]{2,1,0:T(8,128)(2,1)}, bf16[32,8,1024]{2,1,0:T(8,128)(2,1)S(1)}, u32[]{:S(2)}, u32[]{:S(2)}) collective-permute-start(bf16[32,8,1024]{2,1,0:T(8,128)(2,1)} %param.4), channel_id=1, source_target_pairs={{0,4},{4,0},{8,12},{12,8},{16,20},{20,16},{24,28},{28,24},{32,36},... | collective-permute-start | bytes 1572872 | tf_op jit(solution)/shard_map/ppermute | solution.py:465
  4.0 25.1 %collective-permute-start = (bf16[32,8,1024]{2,1,0:T(8,128)(2,1)}, bf16[32,8,1024]{2,1,0:T(8,128)(2,1)S(1)}, u32[]{:S(2)}, u32[]{:S(2)}) collective-permute-start(bf16[32,8,1024]{2,1,0:T(8,128)(2,1)} %param.4), channel_id=1, source_target_pairs={{0,8},{4,12},{8,16},{12,20},{16,24},{20,28},{24,32},{28,36},{32,40... | collective-permute-start | bytes 1572872 | tf_op jit(solution)/shard_map/ppermute | solution.py:465
  5.9 8.7 %copy-start.1 = (f32[1,8,1024]{2,1,0:T(8,128)S(1)}, f32[1,8,1024]{2,1,0:T(8,128)}, u32[]{:S(2)}) copy-start(f32[1,8,1024]{2,1,0:T(8,128)} %param.7) | copy-start | bytes 98308
  5.9 8.7 %copy-start.2 = (s32[1,1024]{1,0:T(1,128)S(1)}, s32[1,1024]{1,0:T(1,128)}, u32[]{:S(2)}) copy-start(s32[1,1024]{1,0:T(1,128)} %refs_0_.1) | copy-start | bytes 12292
  14.6 5.7 %copy-start = (bf16[32,8,1024]{2,1,0:T(8,128)(2,1)S(1)}, bf16[32,8,1024]{2,1,0:T(8,128)(2,1)}, u32[]{:S(2)}) copy-start(bf16[32,8,1024]{2,1,0:T(8,128)(2,1)} %param.4) | copy-start | bytes 1572868
  16.5 18.9 %collective-permute-start.2 = (bf16[32,8,1024]{2,1,0:T(8,128)(2,1)S(1)}, bf16[32,8,1024]{2,1,0:T(8,128)(2,1)S(1)}, u32[]{:S(2)}, u32[]{:S(2)}) collective-permute-start(bf16[32,8,1024]{2,1,0:T(8,128)(2,1)S(1)} %collective-permute-done.1), channel_id=1, source_target_pairs={{0,8},{8,16},{16,24},{24,32},{32,40},{40,48},{48,56},{56,64},{64,7... | collective-permute-start | bytes 1572872 | tf_op jit(solution)/shard_map/ppermute | solution.py:465
  23.5 3.6 %collective-permute-start.5 = (bf16[32,512]{1,0:T(8,128)(2,1)S(1)}, bf16[32,512]{1,0:T(8,128)(2,1)S(1)}, u32[]{:S(2)}, u32[]{:S(2)}) collective-permute-start(bf16[32,512]{1,0:T(8,128)(2,1)S(1)} %get-tuple-element.44), channel_id=1, source_target_pairs={{0,3},{1,2},{2,1},{3,0},{4,7},{5,6},{6,5},{7,4},{8,11},{9,10},{10,... | collective-permute-start | bytes 98312 | tf_op jit(solution)/shard_map/ppermute | solution.py:256
  23.6 4.0 %collective-permute-start.4 = (bf16[32,512]{1,0:T(8,128)(2,1)S(1)}, bf16[32,512]{1,0:T(8,128)(2,1)S(1)}, u32[]{:S(2)}, u32[]{:S(2)}) collective-permute-start(bf16[32,512]{1,0:T(8,128)(2,1)S(1)} %get-tuple-element.44), channel_id=1, source_target_pairs={{0,2},{1,3},{2,0},{3,1},{4,6},{5,7},{6,4},{7,5},{8,10},{9,11},{10,... | collective-permute-start | bytes 98312 | tf_op jit(solution)/shard_map/ppermute | solution.py:256
  25.0 2.6 %collective-permute-start.3 = (bf16[32,512]{1,0:T(8,128)(2,1)S(1)}, bf16[32,512]{1,0:T(8,128)(2,1)S(1)}, u32[]{:S(2)}, u32[]{:S(2)}) collective-permute-start(bf16[32,512]{1,0:T(8,128)(2,1)S(1)} %get-tuple-element.44), channel_id=1, source_target_pairs={{0,1},{1,0},{2,3},{3,2},{4,5},{5,4},{6,7},{7,6},{8,9},{9,8},{10,11... | collective-permute-start | bytes 98312 | tf_op jit(solution)/shard_map/ppermute | solution.py:256
  39.5 5.7 %collective-permute-start.8 = (bf16[64,512]{1,0:T(8,128)(2,1)S(1)}, bf16[64,512]{1,0:T(8,128)(2,1)S(1)}, u32[]{:S(2)}, u32[]{:S(2)}) collective-permute-start(bf16[64,512]{1,0:T(8,128)(2,1)S(1)} %get-tuple-element.50), channel_id=1, source_target_pairs={{0,3},{1,2},{2,1},{3,0},{4,7},{5,6},{6,5},{7,4},{8,11},{9,10},{10,... | collective-permute-start | bytes 196616 | tf_op jit(solution)/shard_map/ppermute | solution.py:256
  39.5 5.8 %collective-permute-start.7 = (bf16[64,512]{1,0:T(8,128)(2,1)S(1)}, bf16[64,512]{1,0:T(8,128)(2,1)S(1)}, u32[]{:S(2)}, u32[]{:S(2)}) collective-permute-start(bf16[64,512]{1,0:T(8,128)(2,1)S(1)} %get-tuple-element.50), channel_id=1, source_target_pairs={{0,2},{1,3},{2,0},{3,1},{4,6},{5,7},{6,4},{7,5},{8,10},{9,11},{10,... | collective-permute-start | bytes 196616 | tf_op jit(solution)/shard_map/ppermute | solution.py:256
  41.2 4.1 %collective-permute-start.6 = (bf16[64,512]{1,0:T(8,128)(2,1)S(1)}, bf16[64,512]{1,0:T(8,128)(2,1)S(1)}, u32[]{:S(2)}, u32[]{:S(2)}) collective-permute-start(bf16[64,512]{1,0:T(8,128)(2,1)S(1)} %get-tuple-element.50), channel_id=1, source_target_pairs={{0,1},{1,0},{2,3},{3,2},{4,5},{5,4},{6,7},{7,6},{8,9},{9,8},{10,11... | collective-permute-start | bytes 196616 | tf_op jit(solution)/shard_map/ppermute | solution.py:256
  41.4 10.6 %collective-permute-start.11 = (bf16[6,48,1024]{2,1,0:T(8,128)(2,1)S(1)}, bf16[6,48,1024]{2,1,0:T(8,128)(2,1)S(1)}, u32[]{:S(2)}, u32[]{:S(2)}) collective-permute-start(bf16[6,48,1024]{2,1,0:T(8,128)(2,1)S(1)} %get-tuple-element.57), channel_id=1, source_target_pairs={{0,1},{1,2},{2,3},{4,5},{5,6},{6,7},{8,9},{9,10},{10,11},{12,13},{... | collective-permute-start | bytes 1769480 | tf_op jit(solution)/shard_map/ppermute | solution.py:482
  43.6 8.3 %collective-permute-start.12 = (bf16[6,48,1024]{2,1,0:T(8,128)(2,1)S(1)}, bf16[6,48,1024]{2,1,0:T(8,128)(2,1)S(1)}, u32[]{:S(2)}, u32[]{:S(2)}) collective-permute-start(bf16[6,48,1024]{2,1,0:T(8,128)(2,1)S(1)} %get-tuple-element.58), channel_id=1, source_target_pairs={{1,0},{2,1},{3,2},{5,4},{6,5},{7,6},{9,8},{10,9},{11,10},{13,12},{... | collective-permute-start | bytes 1769480 | tf_op jit(solution)/shard_map/ppermute | solution.py:483
  46.9 10.7 %collective-permute-start.9 = (bf16[6,64,1024]{2,1,0:T(8,128)(2,1)S(1)}, bf16[6,64,1024]{2,1,0:T(8,128)(2,1)S(1)}, u32[]{:S(2)}, u32[]{:S(2)}) collective-permute-start(bf16[6,64,1024]{2,1,0:T(8,128)(2,1)S(1)} %get-tuple-element.54), channel_id=1, source_target_pairs={{0,1},{1,2},{2,3},{4,5},{5,6},{6,7},{8,9},{9,10},{10,11},{12,13},{... | collective-permute-start | bytes 2359304 | tf_op jit(solution)/shard_map/ppermute | solution.py:488
  50.7 6.9 %collective-permute-start.10 = (bf16[6,64,1024]{2,1,0:T(8,128)(2,1)S(1)}, bf16[6,64,1024]{2,1,0:T(8,128)(2,1)S(1)}, u32[]{:S(2)}, u32[]{:S(2)}) collective-permute-start(bf16[6,64,1024]{2,1,0:T(8,128)(2,1)S(1)} %get-tuple-element.55), channel_id=1, source_target_pairs={{1,0},{2,1},{3,2},{5,4},{6,5},{7,6},{9,8},{10,9},{11,10},{13,12},{... | collective-permute-start | bytes 2359304 | tf_op jit(solution)/shard_map/ppermute | solution.py:488
  71.6 9.8 %collective-permute-start.15 = (bf16[96,512]{1,0:T(8,128)(2,1)S(1)}, bf16[96,512]{1,0:T(8,128)(2,1)S(1)}, u32[]{:S(2)}, u32[]{:S(2)}) collective-permute-start(bf16[96,512]{1,0:T(8,128)(2,1)S(1)} %get-tuple-element.66), channel_id=1, source_target_pairs={{0,3},{1,2},{2,1},{3,0},{4,7},{5,6},{6,5},{7,4},{8,11},{9,10},{10,... | collective-permute-start | bytes 294920 | tf_op jit(solution)/shard_map/ppermute | solution.py:256
  74.1 11.6 %collective-permute-start.14 = (bf16[96,512]{1,0:T(8,128)(2,1)S(1)}, bf16[96,512]{1,0:T(8,128)(2,1)S(1)}, u32[]{:S(2)}, u32[]{:S(2)}) collective-permute-start(bf16[96,512]{1,0:T(8,128)(2,1)S(1)} %get-tuple-element.66), channel_id=1, source_target_pairs={{0,2},{1,3},{2,0},{3,1},{4,6},{5,7},{6,4},{7,5},{8,10},{9,11},{10,... | collective-permute-start | bytes 294920 | tf_op jit(solution)/shard_map/ppermute | solution.py:256
  81.4 4.2 %collective-permute-start.13 = (bf16[96,512]{1,0:T(8,128)(2,1)S(1)}, bf16[96,512]{1,0:T(8,128)(2,1)S(1)}, u32[]{:S(2)}, u32[]{:S(2)}) collective-permute-start(bf16[96,512]{1,0:T(8,128)(2,1)S(1)} %get-tuple-element.66), channel_id=1, source_target_pairs={{0,1},{1,0},{2,3},{3,2},{4,5},{5,4},{6,7},{7,6},{8,9},{9,8},{10,11... | collective-permute-start | bytes 294920 | tf_op jit(solution)/shard_map/ppermute | solution.py:256
